TPU v7x, 128 devices: a whole 4x4x4 slice. The times are simulated.
128 devices in a mesh: copy: 2 (over x_hi), ctx: 32 (over y, z, x_lo), tp: 2 (over core).
Axes of the slice: x: 4 (x_hi: 2, x_lo: 2; x = x_hi * 2 + x_lo), y: 4, z: 4, core: 2. Of those that a mesh axis runs over, the one named last changes fastest.
Arguments:
- clean_tokens: bfloat16 [8192, 4096], P('ctx', 'copy'), may hold values from -36 to 36
- norm_gain: bfloat16 [4096], replicated, may hold values from 0.5 to 1.5
- mask_embed: bfloat16 [4096], replicated, may hold values from -6 to 6
- time_shift: float32 [4096], replicated, may hold values from -0.5 to 0.5
- w_query: bfloat16 [4096, 2048], P(None, 'tp'), may hold values from -0.09375 to 0.09375
- w_key: bfloat16 [4096, 512], P(None, 'tp'), may hold values from -0.09375 to 0.09375
- w_value: bfloat16 [4096, 512], P(None, 'tp'), may hold values from -0.09375 to 0.09375
- w_out: bfloat16 [2048, 4096], P('tp'), may hold values from -0.125 to 0.125
- q_gain: float32 [128], replicated, may hold values from 2 to 3
- k_gain: float32 [128], replicated, may hold values from 0.5 to 1.5
- masked: int32 [2, 8192], P('copy', 'ctx'), may hold values 0 or 1
- block_live: int32 [2, 128], P('copy', 'ctx'), may hold values 0 or 1
- timesteps: int32 [2], P('copy'), may hold values from 1 to 1000
Outputs:
- clean_out: bfloat16 [8192, 4096], P('ctx', 'tp')
- noised_out: bfloat16 [2, 8192, 4096], P('copy', 'ctx', 'tp')
All inputs are finite; a program needn't handle non-finite values. No bound on the sum of `masked` or of `block_live` on one device may be relied on, other than what follows from the above.
Results may differ from a plain program's by a relative error of at most 0.012.
The roundings to bfloat16 on the way count: a program that leaves them out, or rounds other values in their place, can miss the bound.
Values may be sent and summed in bfloat16 or wider, within the bound.
A program may use at most 320 MiB of HBM per device.

v0:
```python
import math

import jax
import jax.numpy as jnp
from jax import lax
from jax.sharding import PartitionSpec as P

HD = 128
BLK = 64
TSTEPS = 1000


EPS = 1e-06


def inverse_rms(values):
    return lax.rsqrt(jnp.mean(values * values, axis=-1, keepdims=True) + EPS)


def key_terms(state, queries, query_start, key_piece, value_piece, key_start):
    numerator, denominator = state
    streams_count, row_count, kv_local, group_size, head_dim = queries.shape
    piece_rows = key_piece.shape[0]
    key_heads = key_piece.reshape(piece_rows, kv_local, head_dim)
    value_heads = value_piece.reshape(piece_rows, kv_local, head_dim)

    def compute():
        scores = jnp.einsum(
            "srhgd,khd->srhgk", queries, key_heads, preferred_element_type=jnp.float32
        ) * (1.0 / math.sqrt(head_dim))
        query_blocks = (query_start + jnp.arange(row_count, dtype=jnp.int32)) // BLK
        key_blocks = jnp.arange(piece_rows, dtype=jnp.int32) // BLK
        offset = jnp.minimum(jnp.arange(streams_count, dtype=jnp.int32), 1)
        allowed = key_blocks[None, None, :] + offset[:, None, None] <= query_blocks[None, :, None]
        weights = jnp.where(allowed[:, :, None, None, :], jnp.exp(scores), 0.0)
        updated = jnp.einsum(
            "srhgk,khd->srhgd",
            weights.astype(jnp.bfloat16),
            value_heads,
            preferred_element_type=jnp.float32,
        )
        return (updated, jnp.sum(weights, axis=4))

    def unchanged():
        return (numerator, denominator)

    needed = key_start // BLK <= (query_start + row_count - 1) // BLK
    return lax.cond(needed, compute, unchanged)


def own_block(queries, key_heads, value_heads):
    copies, row_count, kv_local, group_size, head_dim = queries.shape
    count_blocks = row_count // BLK
    query_blocks = queries.reshape(copies, count_blocks, BLK, kv_local, group_size, head_dim)
    key_blocks = key_heads.reshape(copies, count_blocks, BLK, kv_local, head_dim)
    value_blocks = value_heads.reshape(copies, count_blocks, BLK, kv_local, head_dim)
    scores = jnp.einsum(
        "cbqhgd,cbkhd->cbqhgk", query_blocks, key_blocks, preferred_element_type=jnp.float32
    ) * (1.0 / math.sqrt(head_dim))
    weights = jnp.exp(scores)
    numerator = jnp.einsum(
        "cbqhgk,cbkhd->cbqhgd",
        weights.astype(jnp.bfloat16),
        value_blocks,
        preferred_element_type=jnp.float32,
    )
    denominator = jnp.sum(weights, axis=5)
    return (
        numerator.reshape(copies, row_count, kv_local, group_size, head_dim),
        denominator.reshape(copies, row_count, kv_local, group_size),
    )


def on_device(
    clean_tokens,
    norm_gain,
    mask_embed,
    time_shift,
    w_query,
    w_key,
    w_value,
    w_out,
    q_gain,
    k_gain,
    masked,
    block_live,
    timesteps,
):
    features = lax.all_gather(clean_tokens, "copy", axis=1, tiled=True)
    local_rows = features.shape[0]
    width = features.shape[1]
    copies = masked.shape[0]
    streams_count = 1 + copies
    kv_local = w_key.shape[1] // HD
    heads_local = w_query.shape[1] // HD
    group_size = heads_local // kv_local
    features_wide = features.astype(jnp.float32)
    gain_wide = norm_gain.astype(jnp.float32)
    normed_clean = (features_wide * inverse_rms(features_wide) * gain_wide).astype(jnp.bfloat16)
    noisy_tokens = jnp.where(
        masked[:, :, None] == 1, mask_embed[None, None, :], features[None, :, :]
    )
    noisy_wide = noisy_tokens.astype(jnp.float32)
    condition = (
        1.0 + timesteps.astype(jnp.float32)[:, None, None] / TSTEPS * time_shift[None, None, :]
    )
    normed_noisy = (noisy_wide * inverse_rms(noisy_wide) * gain_wide * condition).astype(
        jnp.bfloat16
    )
    all_rows = jnp.concatenate([normed_clean[None], normed_noisy], axis=0).reshape(-1, width)
    query_wide = jnp.dot(all_rows, w_query, preferred_element_type=jnp.float32).reshape(
        streams_count, local_rows, kv_local, group_size, HD
    )
    queries = (query_wide * inverse_rms(query_wide) * q_gain).astype(jnp.bfloat16)
    key_wide = jnp.dot(all_rows, w_key, preferred_element_type=jnp.float32).reshape(
        streams_count, local_rows, kv_local, HD
    )
    key_heads = (key_wide * inverse_rms(key_wide) * k_gain).astype(jnp.bfloat16)
    value_heads = (
        jnp.dot(all_rows, w_value, preferred_element_type=jnp.float32)
        .astype(jnp.bfloat16)
        .reshape(streams_count, local_rows, kv_local, HD)
    )
    clean_keys = key_heads[0].reshape(local_rows, kv_local * HD)
    clean_values = value_heads[0].reshape(local_rows, kv_local * HD)
    position = lax.axis_index("ctx")
    first_row = position * local_rows
    groups = ((queries, first_row, key_heads[1:], value_heads[1:]),)
    initial = tuple(
        (
            (jnp.zeros(member[0].shape, jnp.float32), jnp.zeros(member[0].shape[:-1], jnp.float32))
            for member in groups
        )
    )
    piece = (
        lax.all_gather(clean_keys, "ctx", axis=0, tiled=True),
        lax.all_gather(clean_values, "ctx", axis=0, tiled=True),
    )
    key_start = jnp.int32(0)
    totals = tuple(
        (
            key_terms(
                initial[number], groups[number][0], groups[number][1], piece[0], piece[1], key_start
            )
            for number in range(len(groups))
        )
    )
    number = 0
    numerator, denominator = totals[number]
    member = groups[number]
    self_numerator, own_den = own_block(member[0][1:], member[2], member[3])
    numerator = jnp.concatenate([numerator[:1], numerator[1:] + self_numerator], axis=0)
    denominator = jnp.concatenate([denominator[:1], denominator[1:] + own_den], axis=0)
    results = (numerator / denominator[..., None]).astype(jnp.bfloat16)
    head_rows = results.reshape(streams_count * local_rows, heads_local * HD)
    mixed = lax.psum_scatter(
        jnp.dot(head_rows, w_out, preferred_element_type=jnp.float32),
        "tp",
        scatter_dimension=1,
        tiled=True,
    )
    clean_out = mixed[:local_rows].astype(jnp.bfloat16)
    live_rows = jnp.repeat(block_live, BLK, axis=1).astype(jnp.float32)
    noised_out = (
        mixed[local_rows:].reshape(copies, local_rows, -1) * live_rows[:, :, None]
    ).astype(jnp.bfloat16)
    return (clean_out, noised_out)


def solution(mesh):
    in_specs = (
        P("ctx", "copy"),
        P(),
        P(),
        P(),
        P(None, "tp"),
        P(None, "tp"),
        P(None, "tp"),
        P("tp", None),
        P(),
        P(),
        P("copy", "ctx"),
        P("copy", "ctx"),
        P("copy"),
    )
    out_specs = (P("ctx", "tp"), P("copy", "ctx", "tp"))
    return jax.shard_map(
        on_device, mesh=mesh, in_specs=in_specs, out_specs=out_specs, check_vma=False
    )
```

profile of v0, /device:TPU:121, one launch (start us, length us, event | category | flops | bytes accessed | tf_op | source)
XLA Modules:
  0.0 563.7 jit_solution(7580052467397267353)
XLA Ops:
  7.3 0.7 all-gather.4.cloned.1.call-update
  8.6 0.7 convert_element_type.72
  9.3 4.1 copy.93
  13.5 34.4 %all-gather.4.cloned.1.call-done = bf16[256,4096]{1,0:T(8,128)(2,1)} async-done(((bf16[256,2048]{1,0:T(8,128)(2,1)}), bf16[256,4096]{1,0:T(8,128)(2,1)}) %all-gather.4.cloned.1.call-update) | async-done | bytes 2097168 | tf_op jit(solution)/shard_map/all_gather | solution.py:89
  47.9 3.4 fusion.19
  51.3 4.2 fusion.31
  55.5 1.3 multiply_reduce_fusion.1
  56.8 0.6 copy-done.4
  57.6 0.7 copy.66
  58.5 2.6 pad_maximum_fusion
  61.1 1.3 convolution_convert_fusion
  62.4 0.7 fusion.43
  63.1 11.4 %copy.94 = bf16[1024,4096]{1,0:T(8,128)(2,1)} copy(bf16[1024,4096]{0,1:T(8,128)(2,1)} %bitcast.72) | data formatting | bytes 16777216 | tf_op jit(solution)/shard_map/dot_general | solution.py:111
  74.7 8.1 %multiply_reduce_fusion = (f32[2,256,2,4]{1,3,2,0:T(4,128)S(1)}, f32[2,256,2,4,128]{4,1,3,2,0:T(8,128)S(1)}) fusion(bf16[2,4,128,4096,1]{3,2,1,0,4:T(8,128)(2,1)} %bitcast.73, bf16[1,256,4096]{2,1,0:T(8,128)(2,1)} %copy-done.4, bf16[1,256,4096]{2,1,0:T(8,128)(2,1)S(1)} %copy-done.3), kind=kOutput, calls=%fused_computation.50 | convolution fusion | flops 4304400384 | bytes 14696448 | tf_op jit(solution)/shard_map/dot_general | solution.py:111
  82.9 0.7 multiply_convert_fusion
  83.6 0.7 fusion.46
  85.0 114.7 %all-gather.6.cloned.1.call-done = bf16[8192,256]{1,0:T(8,128)(2,1)} async-done(((bf16[256,256]{1,0:T(8,128)(2,1)}), bf16[8192,256]{1,0:T(8,128)(2,1)}) %all-gather.6.cloned.1.call-update) | async-done | bytes 4194320 | tf_op jit(solution)/shard_map/all_gather | solution.py:136
  199.6 168.3 %all-gather.8.cloned.1.call-done = bf16[8192,256]{1,0:T(8,128)(2,1)} async-done(((bf16[256,256]{1,0:T(8,128)(2,1)}), bf16[8192,256]{1,0:T(8,128)(2,1)}) %all-gather.8.cloned.1.call-update) | async-done | bytes 4194320 | tf_op jit(solution)/shard_map/all_gather | solution.py:137
  368.0 126.5 %conditional.1 = (f32[2,256,2,4,128]{4,1,3,0,2:T(8,128)S(1)}, f32[2,256,2,4]{1,3,0,2:T(4,128)S(1)}) conditional(s32[]{:T(128)} %convert_element_type.70, () %tuple.16, (s32[]{:T(128)}, bf16[8192,256]{1,0:T(8,128)(2,1)}, bf16[2,256,2,4,128]{4,1,3,2,0:T(8,128)(2,1)}, bf16[8192,256]{1,0:T(8,128)(2,1)}) %tuple.45), branch_computations={%region_4.5_spmd, %region_5.7_spmd} | conditional | flops 17385472000 | bytes 313739328 | solution.py:48
  368.1 7.8 %broadcast_compare_fusion = pred[2,256,8192]{1,2,0:T(8,128)(4,1)} fusion(s32[256]{0:T(256)S(1)} %and_select_fusion, s32[2,8192]{1,0:T(2,128)S(1)} %broadcast_add_fusion), kind=kLoop, calls=%fused_computation.5 | loop fusion | flops 4194304 | bytes 4260864 | tf_op jit(solution)/shard_map/cond/branch_1_fun/le | solution.py:34
  375.9 7.0 %reshape.217 = bf16[8192,2,128]{2,1,0:T(2,128)(2,1)} reshape(bf16[8192,256]{1,0:T(8,128)(2,1)} %get-tuple-element.11) | data formatting | bytes 8388608 | tf_op jit(solution)/shard_map/reshape | solution.py:24
  383.0 48.1 %fusion = (f32[2,256,2,4]{1,3,0,2:T(4,128)S(1)}, f32[2,8192,2,256,4]{3,1,4,2,0:T(8,128)}) fusion(pred[2,256,8192]{1,2,0:T(8,128)(4,1)} %broadcast_compare_fusion, bf16[2,256,2,4,128]{4,1,3,2,0:T(8,128)(2,1)S(1)} %copy-done.6, bf16[8192,2,128,1,1]{2,1,0,4,3:T(2,128)(2,1)} %bitcast.74), kind=kOutput, calls=%fused_computation.1 | convolution fusion | flops 8690593792 | bytes 143671296 | tf_op jit(solution)/shard_map/cond/branch_1_fun/srhgd,khd->srhgk/dot_general | solution.py:28
  431.1 6.9 %reshape.218 = bf16[8192,2,128]{2,1,0:T(2,128)(2,1)} reshape(bf16[8192,256]{1,0:T(8,128)(2,1)} %get-tuple-element.13) | data formatting | bytes 8388608 | tf_op jit(solution)/shard_map/reshape | solution.py:25
  438.0 56.5 %fusion.8 = f32[2,256,2,4,128]{4,1,3,0,2:T(8,128)S(1)} fusion(bf16[8192,2,128,1,1]{2,1,0,4,3:T(2,128)(2,1)} %bitcast.75, f32[2,8192,2,256,4]{3,1,4,2,0:T(8,128)} %get-tuple-element.39, pred[2,256,8192]{1,2,0:T(8,128)(4,1)} %broadcast_compare_fusion), kind=kOutput, calls=%fused_computation.9 | convolution fusion | flops 8690597888 | bytes 144703488 | tf_op jit(solution)/shard_map/cond/branch_1_fun/srhgk,khd->srhgd/dot_general | solution.py:36
  494.7 0.7 fusion.33
  495.4 0.8 copy.80
  496.2 0.8 convert_element_type.83
  497.0 10.0 %fusion.47 = f32[512,4096]{1,0:T(8,128)} fusion(bf16[512,1024]{1,0:T(8,128)(2,1)S(1)} %convert_element_type.83, bf16[1024,4096]{1,0:T(8,128)(2,1)} %param.22), kind=kOutput, calls=%fused_computation.80 | convolution fusion | flops 4294967296 | bytes 17825792 | tf_op jit(solution)/shard_map/dot_general | solution.py:157
  507.1 0.6 copy-done.13
  507.9 43.9 %reduce-scatter.2.cloned.1.call-done = f32[512,2048]{1,0:T(8,128)} async-done(((f32[512,4096]{1,0:T(8,128)}), f32[512,2048]{1,0:T(8,128)}) %reduce-scatter.2.cloned.1.call-update) | async-done | bytes 4194320 | tf_op jit(solution)/shard_map/reduce_scatter | solution.py:156
  551.7 2.7 slice.66
  554.4 2.7 fusion.36
  (57 shorter events, 1.7 us)
Async XLA Ops:
  7.2 53.9 %copy-start = (bf16[4096,256]{1,0:T(8,128)(2,1)S(1)}, bf16[4096,256]{1,0:T(8,128)(2,1)}, u32[]{:S(2)}) copy-start(bf16[4096,256]{1,0:T(8,128)(2,1)} %param.21) | copy-start | bytes 6291460
  7.2 6.3 %copy-start.12 = (s32[1,256]{1,0:T(1,128)S(1)}, s32[1,256]{1,0:T(1,128)}, u32[]{:S(2)}) copy-start(s32[1,256]{1,0:T(1,128)} %param.25) | copy-start | bytes 3076
  7.2 6.3 %copy-start.9 = (f32[4096]{0:T(1024)S(1)}, f32[4096]{0:T(1024)}, u32[]{:S(2)}) copy-start(f32[4096]{0:T(1024)} %param.18) | copy-start | bytes 49156
  7.2 40.7 %copy-start.8 = (bf16[4096]{0:T(1024)(128)(2,1)S(1)}, bf16[4096]{0:T(1024)(128)(2,1)}, u32[]{:S(2)}) copy-start(bf16[4096]{0:T(1024)(128)(2,1)} %param.17) | copy-start | bytes 24580
  7.2 40.7 %all-gather.4.cloned.1.call-start = ((), (), s32[]{:S(2)}) async-start(), calls=%async_computation.1 | async-start | bytes 3145728 | tf_op jit(solution)/shard_map/all_gather | solution.py:89
  7.9 191.7 %all-gather.6.cloned.1.call-start = ((), (), s32[]{:S(2)}) async-start(), calls=%async_computation.2 | async-start | bytes 4325376 | tf_op jit(solution)/shard_map/all_gather | solution.py:136
  47.9 7.6 %copy-start.7 = (bf16[256,4096]{1,0:T(8,128)(2,1)S(1)}, bf16[256,4096]{1,0:T(8,128)(2,1)}, u32[]{:S(2)}) copy-start(bf16[256,4096]{1,0:T(8,128)(2,1)} %copy.93) | copy-start | bytes 6291460
  55.5 1.3 copy-start.2
  55.5 2.0 copy-start.4
  55.5 2.0 copy-start.10
  58.4 309.6 %all-gather.8.cloned.1.call-start = ((), (), s32[]{:S(2)}) async-start(), calls=%async_computation.3 | async-start | bytes 4325376 | tf_op jit(solution)/shard_map/all_gather | solution.py:137
  63.1 488.7 %reduce-scatter.2.cloned.1.call-start = ((), (), s32[]{:S(2)}) async-start(), calls=%async_computation.4 | async-start | bytes 12582912 | tf_op jit(solution)/shard_map/reduce_scatter | solution.py:156
  63.1 11.6 %copy-start.3 = (bf16[1,256,4096]{2,1,0:T(8,128)(2,1)S(1)}, bf16[1,256,4096]{2,1,0:T(8,128)(2,1)}, u32[]{:S(2)}) copy-start(bf16[1,256,4096]{2,1,0:T(8,128)(2,1)} %copy-done.2) | copy-start | bytes 6291460
  74.7 8.2 %copy-start.11 = (f32[128]{0:T(128)S(1)}, f32[128]{0:T(128)}, u32[]{:S(2)}) copy-start(f32[128]{0:T(128)} %param.23) | copy-start | bytes 1540
  83.6 1.0 copy-start.5
  375.9 7.0 %copy-start.6 = (bf16[2,256,2,4,128]{4,1,3,2,0:T(8,128)(2,1)S(1)}, bf16[2,256,2,4,128]{4,1,3,2,0:T(8,128)(2,1)}, u32[]{:S(2)}) copy-start(bf16[2,256,2,4,128]{4,1,3,2,0:T(8,128)(2,1)} %get-tuple-element.34) | copy-start | bytes 3145732 | tf_op jit(solution)/shard_map/cond
  507.0 0.7 copy-start.13
  507.7 49.5 %copy-start.1 = (bf16[4096,256]{1,0:T(8,128)(2,1)S(1)}, bf16[4096,256]{1,0:T(8,128)(2,1)}, u32[]{:S(2)}) copy-start(bf16[4096,256]{1,0:T(8,128)(2,1)} %param.21) | copy-start | bytes 6291460
Sparse Core Ops, SparseCore 0:
  9.7 38.1 all-gather.3
  58.5 141.0 all-gather.5
  201.9 166.0 all-gather.7
  507.2 44.4 reduce-scatter.1
where the time goes:
time: 567 us; the launch traced here: 564 us
  waiting for transfers between devices  362 us (64%)
  matrix products  126 us (22%)
  local copies, waits for them, and re-layouts  37.2 us (7%)
  other arithmetic  23.4 us (4%)
  between operations  14.7 us (3%)
    all_gather x1, waiting for transfers between devices, on_device(): lax.all_gather(clean_values, 'ctx', axis=0, tiled=True)  168 us
    all_gather x1, waiting for transfers between devices, on_device(): lax.all_gather(clean_keys, 'ctx', axis=0, tiled=True)  115 us
    dot_general x1, matrix products, compute(): jnp.einsum('srhgk,khd->srhgd', weights.astype(jnp.bfloat16), value_heads,...  56.5 us
    dot_general x1, matrix products, compute(): jnp.einsum('srhgd,khd->srhgk', queries, key_heads, preferred_element_type...  48.1 us
    reduce_scatter x1, waiting for transfers between devices, on_device(): lax.psum_scatter(jnp.dot(head_rows, w_out, preferred_element_type=jnp.flo...  43.9 us
    all_gather x1, waiting for transfers between devices, on_device(): features = lax.all_gather(clean_tokens, 'copy', axis=1, tiled=True)  34.4 us
    dot_general x1, local copies, waits for them, and re-layouts, on_device(): jnp.dot(all_rows, w_query, preferred_element_type=jnp.float32)  11.4 us
  transfers between devices with their start and end apart: 4, of which 4 were waited for; matrix products, arithmetic and copies ran while one was open for 6% of the time, Pallas kernels for 0%

commit v1 on v0

v1 whole, which is shorter than its diff:
```python
import functools
import math

import jax
import jax.numpy as jnp
from jax import lax
from jax.experimental import pallas as pl
from jax.experimental.pallas import tpu as pltpu
from jax.sharding import PartitionSpec as P

HD = 128
BLK = 64
TSTEPS = 1000
EPS = 1e-06
GROUP = 4


def inverse_rms(values):
    return lax.rsqrt(jnp.mean(values * values, axis=-1, keepdims=True) + EPS)


def attend_kernel(rows, heads, streams, raw_ref, gain_ref, own_ref, kv_ref, out_ref, q_ref, acc_ref):
    me = lax.axis_index("ctx")
    scale = math.log2(math.e) / math.sqrt(HD)
    gain = gain_ref[...]
    query_block = lax.broadcasted_iota(jnp.int32, (rows, rows), 0) // BLK
    key_block = lax.broadcasted_iota(jnp.int32, (rows, rows), 1) // BLK

    def split(kv):
        ones = jnp.ones((kv.shape[0], HD), jnp.bfloat16)
        return kv[:, :HD], jnp.concatenate([kv[:, HD:], ones], axis=1)

    def exponentials(queries, keys):
        scores = lax.dot_general(
            queries, keys, (((1,), (1,)), ((), ())), preferred_element_type=jnp.float32
        )
        return jnp.exp2(scores * scale)

    keys, values = split(own_ref[0])
    for stream in range(streams):
        if stream:
            self_keys, self_values = split(own_ref[stream])
        for head in range(heads):
            raw = raw_ref[stream * rows : (stream + 1) * rows, head * HD : (head + 1) * HD]
            queries = (raw * inverse_rms(raw) * gain).astype(jnp.bfloat16)
            at = pl.ds((stream * heads + head) * rows, rows)
            q_ref[at] = queries
            allowed = key_block < query_block if stream else key_block <= query_block
            weights = jnp.where(allowed, exponentials(queries, keys), 0.0).astype(jnp.bfloat16)
            total = jnp.dot(weights, values, preferred_element_type=jnp.float32)
            if stream:
                weights = jnp.where(
                    key_block == query_block, exponentials(queries, self_keys), 0.0
                ).astype(jnp.bfloat16)
                total += jnp.dot(weights, self_values, preferred_element_type=jnp.float32)
            acc_ref[at] = total

    def accumulate(start, count):
        group_keys, group_values = split(kv_ref[pl.ds(start, count)].reshape(count * rows, 2 * HD))
        for tile in range(streams * heads):
            at = pl.ds(tile * rows, rows)
            weights = exponentials(q_ref[at], group_keys).astype(jnp.bfloat16)
            acc_ref[at] += jnp.dot(weights, group_values, preferred_element_type=jnp.float32)

    def whole(step, carry):
        accumulate(step * GROUP, GROUP)
        return carry

    def single(step, carry):
        accumulate(step, 1)
        return carry

    lax.fori_loop(0, me // GROUP, whole, 0)
    lax.fori_loop(me // GROUP * GROUP, me, single, 0)
    for stream in range(streams):
        for head in range(heads):
            at = pl.ds((stream * heads + head) * rows, rows)
            out_ref[stream * rows : (stream + 1) * rows, head * HD : (head + 1) * HD] = (
                acc_ref[at, :HD] / acc_ref[at, HD:]
            ).astype(jnp.bfloat16)


def attend(raw, q_gain, own, kv, streams, rows, heads):
    return pl.pallas_call(
        functools.partial(attend_kernel, rows, heads, streams),
        out_shape=jax.ShapeDtypeStruct((streams * rows, heads * HD), jnp.bfloat16),
        in_specs=[pl.BlockSpec(memory_space=pltpu.VMEM)] * 4,
        out_specs=pl.BlockSpec(memory_space=pltpu.VMEM),
        scratch_shapes=[
            pltpu.VMEM((streams * heads * rows, HD), jnp.bfloat16),
            pltpu.VMEM((streams * heads * rows, 2 * HD), jnp.float32),
        ],
        compiler_params=pltpu.CompilerParams(vmem_limit_bytes=48 * 2**20),
    )(raw, q_gain, own, kv)


SWAP = [(0, 1), (1, 0)]


def on_device(
    clean_tokens,
    norm_gain,
    mask_embed,
    time_shift,
    w_query,
    w_key,
    w_value,
    w_out,
    q_gain,
    k_gain,
    masked,
    block_live,
    timesteps,
):
    mine = lax.axis_index("copy")
    core = lax.axis_index("tp")
    first = mine == 0
    rows = clean_tokens.shape[0]
    streams = 3
    q_width = w_query.shape[1] // 2
    heads = q_width // HD

    def ordered(own, other, axis):
        return jnp.where(
            first,
            jnp.concatenate([own, other], axis=axis),
            jnp.concatenate([other, own], axis=axis),
        )

    notes = jnp.concatenate([masked, timesteps[:, None]], axis=1)
    other_notes = lax.ppermute(notes, "copy", SWAP)
    other_tokens = lax.ppermute(clean_tokens, "copy", SWAP)
    weights = jnp.concatenate(
        [
            lax.dynamic_slice_in_dim(w_query, mine * q_width, q_width, axis=1),
            lax.dynamic_slice_in_dim(w_key, mine * HD, HD, axis=1),
            lax.dynamic_slice_in_dim(w_value, mine * HD, HD, axis=1),
        ],
        axis=1,
    )
    features = ordered(clean_tokens, other_tokens, 1).astype(jnp.float32)
    both_notes = ordered(notes, other_notes, 0)
    gain = norm_gain.astype(jnp.float32)
    base = features * inverse_rms(features) * gain
    mask_wide = mask_embed.astype(jnp.float32)[None, :]
    mask_base = mask_wide * inverse_rms(mask_wide) * gain
    condition = (
        1.0 + both_notes[:, rows:].astype(jnp.float32)[:, :, None] / TSTEPS * time_shift[None, None, :]
    )
    noisy = jnp.where(both_notes[:, :rows, None] == 1, mask_base[None], base[None]) * condition
    all_rows = jnp.concatenate([base[None], noisy], axis=0).astype(jnp.bfloat16)
    wide = jnp.dot(
        all_rows.reshape(streams * rows, -1), weights, preferred_element_type=jnp.float32
    )
    raw = wide[:, :q_width]
    key_wide = wide[:, q_width : q_width + HD]
    keys = (key_wide * inverse_rms(key_wide) * k_gain).astype(jnp.bfloat16)
    values = wide[:, q_width + HD :].astype(jnp.bfloat16)
    own = jnp.concatenate([keys, values], axis=1).reshape(streams, rows, 2 * HD)
    kv = lax.all_gather(own[0], "ctx", axis=0)
    attended = attend(raw, q_gain[None, :], own, kv, streams, rows, heads)
    attended = attended.reshape(streams, rows, q_width)
    kept = jnp.concatenate(
        [attended[:1], lax.dynamic_slice_in_dim(attended, 1 + mine, 1, axis=0)], axis=0
    )
    given = jnp.concatenate(
        [attended[:1], lax.dynamic_slice_in_dim(attended, 2 - mine, 1, axis=0)], axis=0
    )
    taken = lax.ppermute(given, "copy", SWAP)
    head_rows = ordered(kept, taken, 2).reshape(2 * rows, 2 * q_width)
    half = w_out.shape[1] // 2
    away = lax.dynamic_slice_in_dim(w_out, (1 - core) * half, half, axis=1)
    here = lax.dynamic_slice_in_dim(w_out, core * half, half, axis=1)
    sent = jnp.dot(head_rows, away, preferred_element_type=jnp.float32).astype(jnp.bfloat16)
    received = lax.ppermute(sent, "tp", SWAP)
    mixed = jnp.dot(head_rows, here, preferred_element_type=jnp.float32) + received.astype(
        jnp.float32
    )
    clean_out = mixed[:rows].astype(jnp.bfloat16)
    live_rows = jnp.repeat(block_live, BLK, axis=1).astype(jnp.float32)
    noised_out = (mixed[None, rows:] * live_rows[:, :, None]).astype(jnp.bfloat16)
    return (clean_out, noised_out)


def solution(mesh):
    in_specs = (
        P("ctx", "copy"),
        P(),
        P(),
        P(),
        P(None, "tp"),
        P(None, "tp"),
        P(None, "tp"),
        P("tp", None),
        P(),
        P(),
        P("copy", "ctx"),
        P("copy", "ctx"),
        P("copy"),
    )
    out_specs = (P("ctx", "tp"), P("copy", "ctx", "tp"))
    return jax.shard_map(
        on_device, mesh=mesh, in_specs=in_specs, out_specs=out_specs, check_vma=False
    )
```

time: 567 us -> 282 us (0.50)
  waiting for transfers between devices: 362 us -> 164 us
  matrix products: 126 us -> 18.2 us
  Pallas kernels: 0 us -> 31.5 us
  starting transfers between devices: 0.16 us -> 25.2 us
  local copies, waits for them, and re-layouts: 37.2 us -> 17 us
  other arithmetic: 23.4 us -> 8.91 us
    all_gather x3 -> x1, waiting for transfers between devices: 317 us -> 139 us  [on_device(): kv = lax.all_gather(own[0], 'ctx', axis=0)]
    dot_general x8 -> x3, matrix products: 126 us -> 18.2 us  [the longest x1 7.65 us: on_device(): jnp.dot(all_rows.reshape(streams * rows, -1), weights, preferred_element_...]
    reduce_scatter x1 -> x0, waiting for transfers between devices: 43.9 us -> none  [on_device(): lax.psum_scatter(jnp.dot(head_rows, w_out, preferred_element_type=jnp.flo...]
    pallas_call x0 -> x1, Pallas kernels: none -> 31.5 us  [attend(): pl.pallas_call(functools.partial(attend_kernel, rows, heads, streams), ou...]
    ppermute x0 -> x4, starting transfers between devices: none -> 25.2 us  [the longest x1 19.6 us: on_device(): received = lax.ppermute(sent, 'tp', SWAP)]
    ppermute x0 -> x4, waiting for transfers between devices: none -> 24.6 us  [the longest x1 13.7 us: on_device(): other_notes = lax.ppermute(notes, 'copy', SWAP)]
    dot_general x2 -> x0, local copies, waits for them, and re-layouts: 15.5 us -> none  [the longest x1 11.4 us: on_device(): jnp.dot(all_rows, w_query, preferred_element_type=jnp.float32)]
    reshape x3 -> x0, local copies, waits for them, and re-layouts: 14 us -> none  [the longest x1 7.01 us: key_terms(): key_heads = key_piece.reshape(piece_rows, kv_local, head_dim)]
  transfers between devices with their start and end apart: 4 -> 5, of which waited for: 4 -> 4; matrix products, arithmetic and copies ran while one was open for 6% -> 4% of each run, Pallas kernels for 0% -> 0%
where the time goes in v1:
time: 282 us; the launch traced here: 280 us
  waiting for transfers between devices  164 us (58%)
  Pallas kernels  31.5 us (11%)
  starting transfers between devices  25.2 us (9%)
  matrix products  18.2 us (6%)
  local copies, waits for them, and re-layouts  17 us (6%)
  between operations  15.6 us (6%)
  other arithmetic  8.91 us (3%)
    all_gather x1, waiting for transfers between devices, on_device(): kv = lax.all_gather(own[0], 'ctx', axis=0)  139 us
    pallas_call x1, Pallas kernels, attend(): pl.pallas_call(functools.partial(attend_kernel, rows, heads, streams), ou...  31.5 us
    ppermute x1, starting transfers between devices, on_device(): received = lax.ppermute(sent, 'tp', SWAP)  19.6 us
    ppermute x1, waiting for transfers between devices, on_device(): other_notes = lax.ppermute(notes, 'copy', SWAP)  13.7 us
    dot_general x1, matrix products, on_device(): jnp.dot(all_rows.reshape(streams * rows, -1), weights, preferred_element_...  7.65 us
    ppermute x1, waiting for transfers between devices, on_device(): taken = lax.ppermute(given, 'copy', SWAP)  7.11 us
    all_gather x1, local copies, waits for them, and re-layouts, on_device(): kv = lax.all_gather(own[0], 'ctx', axis=0)  6.41 us
    dot_general x1, matrix products, on_device(): jnp.dot(head_rows, away, preferred_element_type=jnp.float32)  5.92 us
  transfers between devices with their start and end apart: 5, of which 4 were waited for; matrix products, arithmetic and copies ran while one was open for 4% of the time, Pallas kernels for 0%

profile of v1, /device:TPU:121, one launch (start us, length us, event | category | flops | bytes accessed | tf_op | source)
XLA Modules:
  0.0 280.3 jit_solution(13427811830793516056)
XLA Ops:
  7.2 2.8 %collective-permute-start = (bf16[256,2048]{1,0:T(8,128)(2,1)}, bf16[256,2048]{1,0:T(8,128)(2,1)S(1)}, u32[]{:S(2)}, u32[]{:S(2)}) collective-permute-start(bf16[256,2048]{1,0:T(8,128)(2,1)} %param.13), channel_id=1, source_target_pairs={{0,64},{64,0},{1,65},{65,1},{2,66},{66,2},{3,67},{67,3},{4,68},{68... | collective-permute-start | bytes 3145736 | tf_op jit(solution)/shard_map/ppermute | solution.py:132
  10.7 0.7 pad_add_fusion
  11.4 0.2 collective-permute-start.1
  11.6 1.3 fusion.20
  13.6 4.6 %constant_dynamic-slice_fusion.4 = bf16[4096,512]{1,0:T(8,128)(2,1)} fusion(bf16[4096,1024]{1,0:T(8,128)(2,1)} %param.17, s32[]{:T(128)S(6)} %select_n.68), kind=kLoop, calls=%fused_computation.50 | loop fusion | bytes 8388612 | tf_op jit(solution)/shard_map/dynamic_slice | solution.py:135
  18.3 1.1 constant_dynamic-slice_fusion.2
  19.4 13.7 %collective-permute-done.1 = s32[1,257]{1,0:T(1,128)S(1)} collective-permute-done((s32[1,257]{1,0:T(1,128)S(1)}, s32[1,257]{1,0:T(1,128)S(1)}, u32[]{:S(2)}, u32[]{:S(2)}) %collective-permute-start.1) | collective-permute-done | bytes 1060 | tf_op jit(solution)/shard_map/ppermute | solution.py:131
  33.1 0.1 fusion.25
  33.3 0.6 fusion.6
  34.0 0.9 multiply_convert_fusion.1
  34.9 0.8 fusion.7
  35.7 1.7 multiply_convert_fusion
  37.4 0.5 pad_maximum_fusion
  38.0 7.7 %fusion = f32[768,768]{0,1:T(8,128)S(1)} fusion(bf16[768,4096]{1,0:T(8,128)(2,1)S(1)} %bitcast.25, bf16[4096,128]{1,0:T(8,128)(2,1)S(1)} %get-tuple-element.6, bf16[4096,128]{1,0:T(8,128)(2,1)} %get-tuple-element.7, bf16[4096,512]{1,0:T(8,128)(2,1)} %constant_dynamic-slice_fusion.4), kind=kOutput, calls=%fused_computation.2 | convolution fusion | flops 4850712576 | bytes 14942208 | tf_op jit(solution)/shard_map/dot_general | solution.py:152
  45.8 1.3 copy-done.2
  47.1 0.1 multiply_convert_fusion.2
  47.2 0.7 fusion.19
  47.9 1.5 slice.49
  49.4 0.2 copy.19
  49.6 0.5 copy.21.raw_ref
  50.1 139.3 %all-gather.3.cloned.1.call-done = bf16[8192,256]{0,1:T(8,128)(2,1)} async-done(((bf16[256,256]{0,1:T(8,128)(2,1)}), bf16[8192,256]{0,1:T(8,128)(2,1)}) %all-gather.3.cloned.1.call-update) | async-done | bytes 4194320 | tf_op jit(solution)/shard_map/all_gather | solution.py:160
  189.4 6.4 %copy.20 = bf16[8192,256]{1,0:T(8,128)(2,1)} copy(bf16[8192,256]{0,1:T(8,128)(2,1)} %all-gather.3.cloned.1.call-done) | data formatting | bytes 8388608 | tf_op jit(solution)/shard_map/all_gather | solution.py:160
  195.8 31.5 %shard_map.140 = bf16[768,512]{1,0:T(8,128)(2,1)S(1)} custom-call(f32[768,512]{1,0:T(8,128)S(1)} %copy.21.raw_ref, f32[1,128]{1,0:T(1,128)S(1)} %bitcast.21, bf16[3,256,256]{2,1,0:T(8,128)(2,1)S(1)} %bitcast.20, bf16[32,256,256]{2,1,0:T(8,128)(2,1)} %bitcast.22), custom_call_target="tpu_custom_call" | custom-call | tf_op jit(solution)/shard_map/pallas_call | solution.py:84
  227.5 2.5 collective-permute-start.2
  230.0 7.1 %collective-permute-done.2 = bf16[2,256,512]{2,1,0:T(8,128)(2,1)S(1)} collective-permute-done((bf16[2,256,512]{2,1,0:T(8,128)(2,1)S(1)}, bf16[2,256,512]{2,1,0:T(8,128)(2,1)S(1)}, u32[]{:S(2)}, u32[]{:S(2)}) %collective-permute-start.2) | collective-permute-done | bytes 524320 | tf_op jit(solution)/shard_map/ppermute | solution.py:169
  237.1 5.9 %fusion.14 = bf16[512,2048]{1,0:T(8,128)(2,1)} fusion(bf16[1024,4096]{1,0:T(8,128)(2,1)} %param.20, s32[]{:T(128)S(6)} %select_n.74, bf16[512,512]{1,0:T(8,128)(2,1)S(1)} %bitcast.28, bf16[512,512]{1,0:T(8,128)(2,1)S(1)} %bitcast.26, pred[]{:T(512)S(6)} %eq.10), kind=kOutput, calls=%fused_computation.18 | convolution fusion | flops 2153250816 | bytes 7340037 | tf_op jit(solution)/shard_map/dot_general | solution.py:174
  243.0 19.6 %collective-permute-start.3 = (bf16[512,2048]{1,0:T(8,128)(2,1)}, bf16[512,2048]{1,0:T(8,128)(2,1)S(1)}, u32[]{:S(2)}, u32[]{:S(2)}) collective-permute-start(bf16[512,2048]{1,0:T(8,128)(2,1)} %fusion.14), channel_id=1, source_target_pairs={{0,1},{1,0},{2,3},{3,2},{4,5},{5,4},{6,7},{7,6},{8,9},{9,8},{10,11... | collective-permute-start | bytes 6291464 | tf_op jit(solution)/shard_map/ppermute | solution.py:175
  262.7 0.1 convert_element_type.71
  262.8 3.8 %collective-permute-done.3 = bf16[512,2048]{1,0:T(8,128)(2,1)S(1)} collective-permute-done((bf16[512,2048]{1,0:T(8,128)(2,1)}, bf16[512,2048]{1,0:T(8,128)(2,1)S(1)}, u32[]{:S(2)}, u32[]{:S(2)}) %collective-permute-start.3) | collective-permute-done | bytes 2097184 | tf_op jit(solution)/shard_map/ppermute | solution.py:175
  266.6 4.6 %convert_add_fusion = f32[512,2048]{1,0:T(8,128)S(1)} fusion(bf16[512,2048]{1,0:T(8,128)(2,1)S(1)} %collective-permute-done.3, bf16[1024,4096]{1,0:T(8,128)(2,1)} %param.20, s32[]{:T(128)S(6)} %select_n.73, bf16[512,512]{1,0:T(8,128)(2,1)S(1)} %bitcast.29, bf16[512,512]{1,0:T(8,128)(2,1)S(1)} %bitcast.27, pred[]{:T(512)S(6)} %eq.10), kind=kOutput, calls=%fused_computation.12 | convolution fusion | flops 2154299392 | bytes 11534341 | tf_op jit(solution)/shard_map/dot_general | solution.py:176
  271.2 1.1 slice.79
  272.3 1.1 fusion.18
  (39 shorter events, 0.5 us)
Async XLA Ops:
  7.2 182.3 %all-gather.3.cloned.1.call-start = ((), (), s32[]{:S(2)}) async-start(), calls=%async_computation | async-start | bytes 4325376 | tf_op jit(solution)/shard_map/all_gather | solution.py:160
  7.2 26.1 %collective-permute-start = (bf16[256,2048]{1,0:T(8,128)(2,1)}, bf16[256,2048]{1,0:T(8,128)(2,1)S(1)}, u32[]{:S(2)}, u32[]{:S(2)}) collective-permute-start(bf16[256,2048]{1,0:T(8,128)(2,1)} %param.13), channel_id=1, source_target_pairs={{0,64},{64,0},{1,65},{65,1},{2,66},{66,2},{3,67},{67,3},{4,68},{68... | collective-permute-start | bytes 3145736 | tf_op jit(solution)/shard_map/ppermute | solution.py:132
  11.4 21.7 %collective-permute-start.1 = (s32[1,257]{1,0:T(1,128)S(1)}, s32[1,257]{1,0:T(1,128)S(1)}, u32[]{:S(2)}, u32[]{:S(2)}) collective-permute-start(s32[1,257]{1,0:T(1,128)S(1)} %pad_add_fusion), channel_id=1, source_target_pairs={{0,64},{64,0},{1,65},{65,1},{2,66},{66,2},{3,67},{67,3},{4,68},{68... | collective-permute-start | bytes 3092 | tf_op jit(solution)/shard_map/ppermute | solution.py:131
  13.6 4.6 %copy-start.3 = (bf16[4096,256]{1,0:T(8,128)(2,1)S(1)}, bf16[4096,256]{1,0:T(8,128)(2,1)}, u32[]{:S(2)}) copy-start(bf16[4096,256]{1,0:T(8,128)(2,1)} %param.19) | copy-start | bytes 6291460
  13.6 4.6 %copy-start.4 = (bf16[4096,256]{1,0:T(8,128)(2,1)S(1)}, bf16[4096,256]{1,0:T(8,128)(2,1)}, u32[]{:S(2)}) copy-start(bf16[4096,256]{1,0:T(8,128)(2,1)} %param.18) | copy-start | bytes 6291460
  18.2 1.2 copy-start.5
  18.2 1.2 copy-start.6
  18.2 14.9 %copy-start.8 = (s32[1,256]{1,0:T(1,128)S(1)}, s32[1,256]{1,0:T(1,128)}, u32[]{:S(2)}) copy-start(s32[1,256]{1,0:T(1,128)} %param.23) | copy-start | bytes 3076
  18.2 15.0 %copy-start.7 = (f32[4096]{0:T(1024)S(1)}, f32[4096]{0:T(1024)}, u32[]{:S(2)}) copy-start(f32[4096]{0:T(1024)} %param.16) | copy-start | bytes 49156
  18.2 15.1 %copy-start.1 = (bf16[256,2048]{1,0:T(8,128)(2,1)S(1)}, bf16[256,2048]{1,0:T(8,128)(2,1)}, u32[]{:S(2)}) copy-start(bf16[256,2048]{1,0:T(8,128)(2,1)} %param.13) | copy-start | bytes 3145732
  38.0 9.1 %copy-start.9 = (f32[128]{0:T(128)S(1)}, f32[128]{0:T(128)}, u32[]{:S(2)}) copy-start(f32[128]{0:T(128)} %param.22) | copy-start | bytes 1540
  45.7 1.4 copy-start.2
  50.1 145.8 %copy-start = (f32[128]{0:T(128)S(1)}, f32[128]{0:T(128)}, u32[]{:S(2)}) copy-start(f32[128]{0:T(128)} %param.21) | copy-start | bytes 1540
  227.5 9.6 %collective-permute-start.2 = (bf16[2,256,512]{2,1,0:T(8,128)(2,1)S(1)}, bf16[2,256,512]{2,1,0:T(8,128)(2,1)S(1)}, u32[]{:S(2)}, u32[]{:S(2)}) collective-permute-start(bf16[2,256,512]{2,1,0:T(8,128)(2,1)S(1)} %get-tuple-element.5), channel_id=1, source_target_pairs={{0,64},{64,0},{1,65},{65,1},{2,66},{66,2},{3,67},{67,3},{4,68},{68... | collective-permute-start | bytes 1572872 | tf_op jit(solution)/shard_map/ppermute | solution.py:169
  237.1 25.5 %copy-start.10 = (s32[1,4]{1,0:T(1,128)S(1)}, s32[1,4]{1,0:T(1,128)}, u32[]{:S(2)}) copy-start(s32[1,4]{1,0:T(1,128)} %param.24) | copy-start | bytes 52
  243.0 23.6 %collective-permute-start.3 = (bf16[512,2048]{1,0:T(8,128)(2,1)}, bf16[512,2048]{1,0:T(8,128)(2,1)S(1)}, u32[]{:S(2)}, u32[]{:S(2)}) collective-permute-start(bf16[512,2048]{1,0:T(8,128)(2,1)} %fusion.14), channel_id=1, source_target_pairs={{0,1},{1,0},{2,3},{3,2},{4,5},{5,4},{6,7},{7,6},{8,9},{9,8},{10,11... | collective-permute-start | bytes 6291464 | tf_op jit(solution)/shard_map/ppermute | solution.py:175
Sparse Core Ops, SparseCore 0:
  48.0 141.3 all-gather.2

commit v2 on v1

--- a/solution.py
+++ b/solution.py
@@ -13,14 +13,58 @@
 TSTEPS = 1000
 EPS = 1e-06
 GROUP = 4
+MESH = pl.DeviceIdType.MESH
 
 
 def inverse_rms(values):
     return lax.rsqrt(jnp.mean(values * values, axis=-1, keepdims=True) + EPS)
 
 
-def attend_kernel(rows, heads, streams, raw_ref, gain_ref, own_ref, kv_ref, out_ref, q_ref, acc_ref):
+def attend_kernel(
+    rows, heads, streams, spans, raw_ref, gain_ref, own_ref, out_ref, kv_ref, q_ref, acc_ref, send_sem, recv_sem
+):
     me = lax.axis_index("ctx")
+
+    barrier = pltpu.get_barrier_semaphore()
+
+    def greet(step, carry):
+        pl.semaphore_signal(
+            barrier, inc=1, device_id={"ctx": lax.rem(me + step, spans)}, device_id_type=MESH
+        )
+        return carry
+
+    lax.fori_loop(1, spans, greet, 0)
+    pl.semaphore_wait(barrier, spans - 1)
+
+    def push(target):
+        return pltpu.make_async_remote_copy(
+            src_ref=own_ref.at[0],
+            dst_ref=kv_ref.at[me],
+            send_sem=send_sem.at[target],
+            recv_sem=recv_sem.at[me],
+            device_id={"ctx": target},
+            device_id_type=MESH,
+        )
+
+    def arrival(source):
+        return pltpu.make_async_remote_copy(
+            src_ref=own_ref.at[0],
+            dst_ref=kv_ref.at[source],
+            send_sem=send_sem.at[source],
+            recv_sem=recv_sem.at[source],
+            device_id={"ctx": source},
+            device_id_type=MESH,
+        )
+
+    def start_push(target, carry):
+        push(target).start()
+        return carry
+
+    def end_push(target, carry):
+        push(target).wait_send()
+        return carry
+
+    lax.fori_loop(me + 1, spans, start_push, 0)
     scale = math.log2(math.e) / math.sqrt(HD)
     gain = gain_ref[...]
     query_block = lax.broadcasted_iota(jnp.int32, (rows, rows), 0) // BLK
@@ -56,6 +100,8 @@
             acc_ref[at] = total
 
     def accumulate(start, count):
+        for offset in range(count):
+            arrival(start + offset).wait_recv()
         group_keys, group_values = split(kv_ref[pl.ds(start, count)].reshape(count * rows, 2 * HD))
         for tile in range(streams * heads):
             at = pl.ds(tile * rows, rows)
@@ -63,35 +109,41 @@
             acc_ref[at] += jnp.dot(weights, group_values, preferred_element_type=jnp.float32)
 
     def whole(step, carry):
-        accumulate(step * GROUP, GROUP)
+        accumulate(me - (step + 1) * GROUP, GROUP)
         return carry
 
     def single(step, carry):
-        accumulate(step, 1)
+        accumulate(lax.rem(me, GROUP) - 1 - step, 1)
         return carry
 
     lax.fori_loop(0, me // GROUP, whole, 0)
-    lax.fori_loop(me // GROUP * GROUP, me, single, 0)
+    lax.fori_loop(0, lax.rem(me, GROUP), single, 0)
     for stream in range(streams):
         for head in range(heads):
             at = pl.ds((stream * heads + head) * rows, rows)
             out_ref[stream * rows : (stream + 1) * rows, head * HD : (head + 1) * HD] = (
                 acc_ref[at, :HD] / acc_ref[at, HD:]
             ).astype(jnp.bfloat16)
-
-
-def attend(raw, q_gain, own, kv, streams, rows, heads):
+    lax.fori_loop(me + 1, spans, end_push, 0)
+
+
+def attend(raw, q_gain, own, streams, rows, heads, spans):
     return pl.pallas_call(
-        functools.partial(attend_kernel, rows, heads, streams),
+        functools.partial(attend_kernel, rows, heads, streams, spans),
         out_shape=jax.ShapeDtypeStruct((streams * rows, heads * HD), jnp.bfloat16),
-        in_specs=[pl.BlockSpec(memory_space=pltpu.VMEM)] * 4,
+        in_specs=[pl.BlockSpec(memory_space=pltpu.VMEM)] * 3,
         out_specs=pl.BlockSpec(memory_space=pltpu.VMEM),
         scratch_shapes=[
+            pltpu.VMEM((spans, rows, 2 * HD), jnp.bfloat16),
             pltpu.VMEM((streams * heads * rows, HD), jnp.bfloat16),
             pltpu.VMEM((streams * heads * rows, 2 * HD), jnp.float32),
+            pltpu.SemaphoreType.DMA((spans,)),
+            pltpu.SemaphoreType.DMA((spans,)),
         ],
-        compiler_params=pltpu.CompilerParams(vmem_limit_bytes=48 * 2**20),
-    )(raw, q_gain, own, kv)
+        compiler_params=pltpu.CompilerParams(
+            vmem_limit_bytes=48 * 2**20, collective_id=0, has_side_effects=True
+        ),
+    )(raw, q_gain, own)
 
 
 SWAP = [(0, 1), (1, 0)]
@@ -157,8 +209,8 @@
     keys = (key_wide * inverse_rms(key_wide) * k_gain).astype(jnp.bfloat16)
     values = wide[:, q_width + HD :].astype(jnp.bfloat16)
     own = jnp.concatenate([keys, values], axis=1).reshape(streams, rows, 2 * HD)
-    kv = lax.all_gather(own[0], "ctx", axis=0)
-    attended = attend(raw, q_gain[None, :], own, kv, streams, rows, heads)
+    spans = lax.axis_size("ctx")
+    attended = attend(raw, q_gain[None, :], own, streams, rows, heads, spans)
     attended = attended.reshape(streams, rows, q_width)
     kept = jnp.concatenate(
         [attended[:1], lax.dynamic_slice_in_dim(attended, 1 + mine, 1, axis=0)], axis=0

time: 282 us -> 151 us (0.54)
  the two profiles are of different devices: /device:TPU:121 before, /device:TPU:89 now
where the time goes in v2:
time: 151 us; the launch traced here: 150 us
  Pallas kernels  76.9 us (51%)
  waiting for transfers between devices  29.1 us (19%)
  matrix products  18.7 us (12%)
  other arithmetic  8.24 us (5%)
  local copies, waits for them, and re-layouts  7.84 us (5%)
  starting transfers between devices  7.36 us (5%)
  between operations  2.24 us (1%)
    pallas_call x1, Pallas kernels, attend(): pl.pallas_call(functools.partial(attend_kernel, rows, heads, streams, spa...  76.9 us
    ppermute x1, waiting for transfers between devices, on_device(): other_notes = lax.ppermute(notes, 'copy', SWAP)  13.7 us
    ppermute x1, waiting for transfers between devices, on_device(): taken = lax.ppermute(given, 'copy', SWAP)  11.6 us
    dot_general x1, matrix products, on_device(): jnp.dot(all_rows.reshape(streams * rows, -1), weights, preferred_element_...  8.17 us
    dot_general x1, matrix products, on_device(): jnp.dot(head_rows, away, preferred_element_type=jnp.float32)  5.92 us
    dot_general x1, matrix products, on_device(): jnp.dot(head_rows, here, preferred_element_type=jnp.float32)  4.6 us
    dynamic_slice x1, local copies, waits for them, and re-layouts, on_device(): lax.dynamic_slice_in_dim(w_query, mine * q_width, q_width, axis=1)  4.56 us
    ppermute x1, waiting for transfers between devices, on_device(): received = lax.ppermute(sent, 'tp', SWAP)  3.83 us
  transfers between devices with their start and end apart: 4, of which 3 were waited for; matrix products, arithmetic and copies ran while one was open for 5% of the time, Pallas kernels for 0%

profile of v2, /device:TPU:89, one launch (start us, length us, event | category | flops | bytes accessed | tf_op | source)
XLA Modules:
  0.0 150.4 jit_solution(456604917154353971)
XLA Ops:
  0.6 2.8 %collective-permute-start = (bf16[256,2048]{1,0:T(8,128)(2,1)}, bf16[256,2048]{1,0:T(8,128)(2,1)S(1)}, u32[]{:S(2)}, u32[]{:S(2)}) collective-permute-start(bf16[256,2048]{1,0:T(8,128)(2,1)} %param.13), channel_id=1, source_target_pairs={{0,64},{64,0},{1,65},{65,1},{2,66},{66,2},{3,67},{67,3},{4,68},{68... | collective-permute-start | bytes 3145736 | tf_op jit(solution)/shard_map/ppermute | solution.py:184
  4.1 0.7 pad_add_fusion
  4.8 0.2 collective-permute-start.1
  5.0 1.3 fusion.19
  7.0 0.0 copy-start.2
  7.0 4.6 %constant_dynamic-slice_fusion.4 = bf16[4096,512]{1,0:T(8,128)(2,1)} fusion(bf16[4096,1024]{1,0:T(8,128)(2,1)} %param.17, s32[]{:T(128)S(6)} %select_n.68), kind=kLoop, calls=%fused_computation.47 | loop fusion | bytes 8388612 | tf_op jit(solution)/shard_map/dynamic_slice | solution.py:187
  11.7 1.1 constant_dynamic-slice_fusion.2
  12.8 13.7 %collective-permute-done.1 = s32[1,257]{1,0:T(1,128)S(1)} collective-permute-done((s32[1,257]{1,0:T(1,128)S(1)}, s32[1,257]{1,0:T(1,128)S(1)}, u32[]{:S(2)}, u32[]{:S(2)}) %collective-permute-start.1) | collective-permute-done | bytes 1060 | tf_op jit(solution)/shard_map/ppermute | solution.py:183
  26.5 0.1 fusion.24
  26.6 0.1 multiply_add_fusion
  26.7 0.6 fusion.6
  27.4 0.9 multiply_convert_fusion.1
  28.3 0.8 fusion.7
  29.1 1.7 %multiply_convert_fusion = bf16[2,256,4096]{2,1,0:T(8,128)(2,1)S(1)} fusion(f32[2,4096]{1,0:T(2,128)S(1)} %multiply_add_fusion, f32[256,4096]{1,0:T(8,128)S(1)} %fusion.7, f32[4096]{0:T(1024)S(1)} %fusion.20, pred[2,256]{1,0:T(4,128)(4,1)S(1)} %slice_compare_fusion), kind=kLoop, calls=%fused_computation | loop fusion | flops 6291456 | bytes 8438272 | tf_op jit(solution)/shard_map/convert.3
  30.8 0.5 pad_maximum_fusion
  31.4 8.2 %fusion = f32[768,768]{0,1:T(8,128)S(1)} fusion(bf16[768,4096]{1,0:T(8,128)(2,1)S(1)} %bitcast.23, bf16[4096,128]{1,0:T(8,128)(2,1)S(1)} %get-tuple-element.6, bf16[4096,128]{1,0:T(8,128)(2,1)} %get-tuple-element.7, bf16[4096,512]{1,0:T(8,128)(2,1)} %constant_dynamic-slice_fusion.4), kind=kOutput, calls=%fused_computation.2 | convolution fusion | flops 4850712576 | bytes 14942208 | tf_op jit(solution)/shard_map/dot_general | solution.py:204
  39.7 0.1 slice.41
  39.8 0.1 multiply_convert_fusion.2
  39.9 0.2 copy.18
  40.1 0.5 copy.19.raw_ref
  40.6 76.9 %shard_map.140 = bf16[768,512]{1,0:T(8,128)(2,1)S(1)} custom-call(f32[768,512]{1,0:T(8,128)S(1)} %copy.19.raw_ref, f32[1,128]{1,0:T(1,128)S(1)} %bitcast.20, bf16[3,256,256]{2,1,0:T(8,128)(2,1)S(1)} %bitcast.19), custom_call_target="tpu_custom_call" | custom-call | tf_op jit(solution)/shard_map/pallas_call | solution.py:131
  117.6 0.1 pad_maximum_fusion.2
  117.7 1.0 collective-permute-start.2
  118.7 11.6 %collective-permute-done.2 = bf16[2,256,512]{2,1,0:T(8,128)(2,1)S(1)} collective-permute-done((bf16[2,256,512]{2,1,0:T(8,128)(2,1)S(1)}, bf16[2,256,512]{2,1,0:T(8,128)(2,1)S(1)}, u32[]{:S(2)}, u32[]{:S(2)}) %collective-permute-start.2) | collective-permute-done | bytes 524320 | tf_op jit(solution)/shard_map/ppermute | solution.py:221
  130.3 5.9 %fusion.14 = bf16[512,2048]{1,0:T(8,128)(2,1)} fusion(bf16[1024,4096]{1,0:T(8,128)(2,1)} %param.20, s32[]{:T(128)S(6)} %select_n.74, bf16[512,512]{1,0:T(8,128)(2,1)S(1)} %bitcast.26, bf16[512,512]{1,0:T(8,128)(2,1)S(1)} %bitcast.24, pred[]{:T(512)S(6)} %eq.10), kind=kOutput, calls=%fused_computation.18 | convolution fusion | flops 2153250816 | bytes 7340037 | tf_op jit(solution)/shard_map/dot_general | solution.py:226
  136.2 3.3 %collective-permute-start.3 = (bf16[512,2048]{1,0:T(8,128)(2,1)}, bf16[512,2048]{1,0:T(8,128)(2,1)S(1)}, u32[]{:S(2)}, u32[]{:S(2)}) collective-permute-start(bf16[512,2048]{1,0:T(8,128)(2,1)} %fusion.14), channel_id=1, source_target_pairs={{0,1},{1,0},{2,3},{3,2},{4,5},{5,4},{6,7},{7,6},{8,9},{9,8},{10,11... | collective-permute-start | bytes 6291464 | tf_op jit(solution)/shard_map/ppermute | solution.py:227
  139.5 0.1 broadcast_in_dim.35
  139.6 0.1 convert_element_type.71
  139.7 3.8 %collective-permute-done.3 = bf16[512,2048]{1,0:T(8,128)(2,1)S(1)} collective-permute-done((bf16[512,2048]{1,0:T(8,128)(2,1)}, bf16[512,2048]{1,0:T(8,128)(2,1)S(1)}, u32[]{:S(2)}, u32[]{:S(2)}) %collective-permute-start.3) | collective-permute-done | bytes 2097184 | tf_op jit(solution)/shard_map/ppermute | solution.py:227
  143.5 4.6 %convert_add_fusion = f32[512,2048]{1,0:T(8,128)S(1)} fusion(bf16[512,2048]{1,0:T(8,128)(2,1)S(1)} %collective-permute-done.3, bf16[1024,4096]{1,0:T(8,128)(2,1)} %param.20, s32[]{:T(128)S(6)} %select_n.73, bf16[512,512]{1,0:T(8,128)(2,1)S(1)} %bitcast.27, bf16[512,512]{1,0:T(8,128)(2,1)S(1)} %bitcast.25, pred[]{:T(512)S(6)} %eq.10), kind=kOutput, calls=%fused_computation.12 | convolution fusion | flops 2154299392 | bytes 11534341 | tf_op jit(solution)/shard_map/dot_general | solution.py:228
  148.1 1.1 slice.62
  149.2 1.1 fusion.18
  (32 shorter events, 0.3 us)
Async XLA Ops:
  0.6 26.1 %collective-permute-start = (bf16[256,2048]{1,0:T(8,128)(2,1)}, bf16[256,2048]{1,0:T(8,128)(2,1)S(1)}, u32[]{:S(2)}, u32[]{:S(2)}) collective-permute-start(bf16[256,2048]{1,0:T(8,128)(2,1)} %param.13), channel_id=1, source_target_pairs={{0,64},{64,0},{1,65},{65,1},{2,66},{66,2},{3,67},{67,3},{4,68},{68... | collective-permute-start | bytes 3145736 | tf_op jit(solution)/shard_map/ppermute | solution.py:184
  4.8 21.7 %collective-permute-start.1 = (s32[1,257]{1,0:T(1,128)S(1)}, s32[1,257]{1,0:T(1,128)S(1)}, u32[]{:S(2)}, u32[]{:S(2)}) collective-permute-start(s32[1,257]{1,0:T(1,128)S(1)} %pad_add_fusion), channel_id=1, source_target_pairs={{0,64},{64,0},{1,65},{65,1},{2,66},{66,2},{3,67},{67,3},{4,68},{68... | collective-permute-start | bytes 3092 | tf_op jit(solution)/shard_map/ppermute | solution.py:183
  7.0 4.6 %copy-start.2 = (bf16[4096,256]{1,0:T(8,128)(2,1)S(1)}, bf16[4096,256]{1,0:T(8,128)(2,1)}, u32[]{:S(2)}) copy-start(bf16[4096,256]{1,0:T(8,128)(2,1)} %param.19) | copy-start | bytes 6291460
  7.0 4.6 %copy-start.3 = (bf16[4096,256]{1,0:T(8,128)(2,1)S(1)}, bf16[4096,256]{1,0:T(8,128)(2,1)}, u32[]{:S(2)}) copy-start(bf16[4096,256]{1,0:T(8,128)(2,1)} %param.18) | copy-start | bytes 6291460
  11.6 1.2 copy-start.4
  11.6 1.2 copy-start.5
  11.6 14.9 %copy-start.7 = (s32[1,256]{1,0:T(1,128)S(1)}, s32[1,256]{1,0:T(1,128)}, u32[]{:S(2)}) copy-start(s32[1,256]{1,0:T(1,128)} %param.23) | copy-start | bytes 3076
  11.6 15.0 %copy-start.6 = (f32[4096]{0:T(1024)S(1)}, f32[4096]{0:T(1024)}, u32[]{:S(2)}) copy-start(f32[4096]{0:T(1024)} %param.16) | copy-start | bytes 49156
  11.6 15.1 %copy-start.1 = (bf16[256,2048]{1,0:T(8,128)(2,1)S(1)}, bf16[256,2048]{1,0:T(8,128)(2,1)}, u32[]{:S(2)}) copy-start(bf16[256,2048]{1,0:T(8,128)(2,1)} %param.13) | copy-start | bytes 3145732
  31.4 8.4 %copy-start.8 = (f32[128]{0:T(128)S(1)}, f32[128]{0:T(128)}, u32[]{:S(2)}) copy-start(f32[128]{0:T(128)} %param.22) | copy-start | bytes 1540
  39.7 0.9 copy-start
  117.7 12.6 %collective-permute-start.2 = (bf16[2,256,512]{2,1,0:T(8,128)(2,1)S(1)}, bf16[2,256,512]{2,1,0:T(8,128)(2,1)S(1)}, u32[]{:S(2)}, u32[]{:S(2)}) collective-permute-start(bf16[2,256,512]{2,1,0:T(8,128)(2,1)S(1)} %get-tuple-element.5), channel_id=1, source_target_pairs={{0,64},{64,0},{1,65},{65,1},{2,66},{66,2},{3,67},{67,3},{4,68},{68... | collective-permute-start | bytes 1572872 | tf_op jit(solution)/shard_map/ppermute | solution.py:221
  130.3 9.2 %copy-start.9 = (s32[1,4]{1,0:T(1,128)S(1)}, s32[1,4]{1,0:T(1,128)}, u32[]{:S(2)}) copy-start(s32[1,4]{1,0:T(1,128)} %param.24) | copy-start | bytes 52
  136.2 7.3 %collective-permute-start.3 = (bf16[512,2048]{1,0:T(8,128)(2,1)}, bf16[512,2048]{1,0:T(8,128)(2,1)S(1)}, u32[]{:S(2)}, u32[]{:S(2)}) collective-permute-start(bf16[512,2048]{1,0:T(8,128)(2,1)} %fusion.14), channel_id=1, source_target_pairs={{0,1},{1,0},{2,3},{3,2},{4,5},{5,4},{6,7},{7,6},{8,9},{9,8},{10,11... | collective-permute-start | bytes 6291464 | tf_op jit(solution)/shard_map/ppermute | solution.py:227

commit v3 on v2

--- a/solution.py
+++ b/solution.py
@@ -21,7 +21,7 @@
 
 
 def attend_kernel(
-    rows, heads, streams, spans, raw_ref, gain_ref, own_ref, out_ref, kv_ref, q_ref, acc_ref, send_sem, recv_sem
+    rows, heads, streams, spans, raw_ref, gain_ref, own_ref, out_ref, kv_ref, q_ref, acc_ref, send_sem, recv_sem, forward_sem
 ):
     me = lax.axis_index("ctx")
 
@@ -56,15 +56,58 @@
             device_id_type=MESH,
         )
 
-    def start_push(target, carry):
-        push(target).start()
-        return carry
-
-    def end_push(target, carry):
-        push(target).wait_send()
-        return carry
-
-    lax.fori_loop(me + 1, spans, start_push, 0)
+    pair = me // 2
+    lane = lax.rem(me, 2)
+    partner = me + 1 - 2 * lane
+
+    def relayed(index):
+        return lax.rem(index, 4) != 3
+
+    def each_push(act):
+        @pl.when(lane == 0)
+        def _():
+            act(push(partner))
+
+        def to_pair(index, carry):
+            act(push(2 * index + lane))
+
+            @pl.when(jnp.logical_not(relayed(pair)))
+            def _():
+                act(push(2 * index + 1 - lane))
+
+            return carry
+
+        lax.fori_loop(pair + 1, spans // 2, to_pair, 0)
+
+    def forward(index):
+        slot = 2 * index + lane
+        return pltpu.make_async_remote_copy(
+            src_ref=kv_ref.at[slot],
+            dst_ref=kv_ref.at[slot],
+            send_sem=forward_sem.at[slot],
+            recv_sem=recv_sem.at[slot],
+            device_id={"ctx": partner},
+            device_id_type=MESH,
+        )
+
+    def relay(step, carry):
+        index = pair - 1 - step
+        arrival(2 * index + lane).wait_recv()
+
+        @pl.when(relayed(index))
+        def _():
+            forward(index).start()
+
+        return carry
+
+    def end_relay(index, carry):
+        @pl.when(relayed(index))
+        def _():
+            forward(index).wait_send()
+
+        return carry
+
+    each_push(lambda copy: copy.start())
     scale = math.log2(math.e) / math.sqrt(HD)
     gain = gain_ref[...]
     query_block = lax.broadcasted_iota(jnp.int32, (rows, rows), 0) // BLK
@@ -100,31 +143,45 @@
             acc_ref[at] = total
 
     def accumulate(start, count):
-        for offset in range(count):
-            arrival(start + offset).wait_recv()
         group_keys, group_values = split(kv_ref[pl.ds(start, count)].reshape(count * rows, 2 * HD))
         for tile in range(streams * heads):
             at = pl.ds(tile * rows, rows)
             weights = exponentials(q_ref[at], group_keys).astype(jnp.bfloat16)
             acc_ref[at] += jnp.dot(weights, group_values, preferred_element_type=jnp.float32)
 
+    pairs = GROUP // 2
+
     def whole(step, carry):
-        accumulate(me - (step + 1) * GROUP, GROUP)
-        return carry
-
-    def single(step, carry):
-        accumulate(lax.rem(me, GROUP) - 1 - step, 1)
-        return carry
-
-    lax.fori_loop(0, me // GROUP, whole, 0)
-    lax.fori_loop(0, lax.rem(me, GROUP), single, 0)
+        lax.fori_loop((step + 1) * pairs, jnp.minimum((step + 2) * pairs, pair), relay, 0)
+        start = pair - (step + 1) * pairs
+        for offset in range(pairs):
+            arrival(2 * (start + offset) + 1 - lane).wait_recv()
+        accumulate(2 * start, GROUP)
+        return carry
+
+    def last(step, carry):
+        index = lax.rem(pair, pairs) - 1 - step
+        arrival(2 * index + 1 - lane).wait_recv()
+        accumulate(2 * index, 2)
+        return carry
+
+    lax.fori_loop(0, jnp.minimum(pairs, pair), relay, 0)
+
+    @pl.when(lane == 1)
+    def _():
+        arrival(2 * pair).wait_recv()
+        accumulate(2 * pair, 1)
+
+    lax.fori_loop(0, pair // pairs, whole, 0)
+    lax.fori_loop(0, lax.rem(pair, pairs), last, 0)
     for stream in range(streams):
         for head in range(heads):
             at = pl.ds((stream * heads + head) * rows, rows)
             out_ref[stream * rows : (stream + 1) * rows, head * HD : (head + 1) * HD] = (
                 acc_ref[at, :HD] / acc_ref[at, HD:]
             ).astype(jnp.bfloat16)
-    lax.fori_loop(me + 1, spans, end_push, 0)
+    each_push(lambda copy: copy.wait_send())
+    lax.fori_loop(0, pair, end_relay, 0)
 
 
 def attend(raw, q_gain, own, streams, rows, heads, spans):
@@ -137,6 +194,7 @@
             pltpu.VMEM((spans, rows, 2 * HD), jnp.bfloat16),
             pltpu.VMEM((streams * heads * rows, HD), jnp.bfloat16),
             pltpu.VMEM((streams * heads * rows, 2 * HD), jnp.float32),
+            pltpu.SemaphoreType.DMA((spans,)),
             pltpu.SemaphoreType.DMA((spans,)),
             pltpu.SemaphoreType.DMA((spans,)),
         ],

time: 151 us -> 142 us (0.940)
  the two profiles are of different devices: /device:TPU:89 before, /device:TPU:121 now
where the time goes in v3:
time: 142 us
  Pallas kernels  68.2 us (48%)
  waiting for transfers between devices  27.3 us (19%)
  matrix products  18.7 us (13%)
  starting transfers between devices  9.23 us (6%)
  other arithmetic  8.24 us (6%)
  local copies, waits for them, and re-layouts  7.84 us (6%)
  between operations  2.24 us (2%)
    pallas_call x1, Pallas kernels, attend(): pl.pallas_call(functools.partial(attend_kernel, rows, heads, streams, spa...  68.2 us
    ppermute x1, waiting for transfers between devices, on_device(): other_notes = lax.ppermute(notes, 'copy', SWAP)  13.7 us
    ppermute x1, waiting for transfers between devices, on_device(): taken = lax.ppermute(given, 'copy', SWAP)  9.74 us
    dot_general x1, matrix products, on_device(): jnp.dot(all_rows.reshape(streams * rows, -1), weights, preferred_element_...  8.17 us
    dot_general x1, matrix products, on_device(): jnp.dot(head_rows, away, preferred_element_type=jnp.float32)  5.92 us
    ppermute x1, starting transfers between devices, on_device(): received = lax.ppermute(sent, 'tp', SWAP)  5.42 us
    dot_general x1, matrix products, on_device(): jnp.dot(head_rows, here, preferred_element_type=jnp.float32)  4.6 us
    dynamic_slice x1, local copies, waits for them, and re-layouts, on_device(): lax.dynamic_slice_in_dim(w_query, mine * q_width, q_width, axis=1)  4.56 us
  transfers between devices with their start and end apart: 4, of which 3 were waited for; matrix products, arithmetic and copies ran while one was open for 6% of the time, Pallas kernels for 0%

profile of v3, /device:TPU:121, one launch (start us, length us, event | category | flops | bytes accessed | tf_op | source)
XLA Modules:
  0.0 141.7 jit_solution(8224095124187025219)
XLA Ops:
  0.6 2.8 %collective-permute-start = (bf16[256,2048]{1,0:T(8,128)(2,1)}, bf16[256,2048]{1,0:T(8,128)(2,1)S(1)}, u32[]{:S(2)}, u32[]{:S(2)}) collective-permute-start(bf16[256,2048]{1,0:T(8,128)(2,1)} %param.13), channel_id=1, source_target_pairs={{0,64},{64,0},{1,65},{65,1},{2,66},{66,2},{3,67},{67,3},{4,68},{68... | collective-permute-start | bytes 3145736 | tf_op jit(solution)/shard_map/ppermute | solution.py:242
  4.1 0.7 pad_add_fusion
  4.8 0.2 collective-permute-start.1
  5.0 1.3 fusion.19
  7.0 0.0 copy-start.2
  7.0 4.6 %constant_dynamic-slice_fusion.4 = bf16[4096,512]{1,0:T(8,128)(2,1)} fusion(bf16[4096,1024]{1,0:T(8,128)(2,1)} %param.17, s32[]{:T(128)S(6)} %select_n.68), kind=kLoop, calls=%fused_computation.47 | loop fusion | bytes 8388612 | tf_op jit(solution)/shard_map/dynamic_slice | solution.py:245
  11.7 1.1 constant_dynamic-slice_fusion.2
  12.8 13.7 %collective-permute-done.1 = s32[1,257]{1,0:T(1,128)S(1)} collective-permute-done((s32[1,257]{1,0:T(1,128)S(1)}, s32[1,257]{1,0:T(1,128)S(1)}, u32[]{:S(2)}, u32[]{:S(2)}) %collective-permute-start.1) | collective-permute-done | bytes 1060 | tf_op jit(solution)/shard_map/ppermute | solution.py:241
  26.5 0.1 fusion.24
  26.6 0.1 multiply_add_fusion
  26.7 0.6 fusion.6
  27.4 0.9 multiply_convert_fusion.1
  28.3 0.8 fusion.7
  29.1 1.7 %multiply_convert_fusion = bf16[2,256,4096]{2,1,0:T(8,128)(2,1)S(1)} fusion(f32[2,4096]{1,0:T(2,128)S(1)} %multiply_add_fusion, f32[256,4096]{1,0:T(8,128)S(1)} %fusion.7, f32[4096]{0:T(1024)S(1)} %fusion.20, pred[2,256]{1,0:T(4,128)(4,1)S(1)} %slice_compare_fusion), kind=kLoop, calls=%fused_computation | loop fusion | flops 6291456 | bytes 8438272 | tf_op jit(solution)/shard_map/convert.3
  30.8 0.5 pad_maximum_fusion
  31.4 8.2 %fusion = f32[768,768]{0,1:T(8,128)S(1)} fusion(bf16[768,4096]{1,0:T(8,128)(2,1)S(1)} %bitcast.23, bf16[4096,128]{1,0:T(8,128)(2,1)S(1)} %get-tuple-element.6, bf16[4096,128]{1,0:T(8,128)(2,1)} %get-tuple-element.7, bf16[4096,512]{1,0:T(8,128)(2,1)} %constant_dynamic-slice_fusion.4), kind=kOutput, calls=%fused_computation.2 | convolution fusion | flops 4850712576 | bytes 14942208 | tf_op jit(solution)/shard_map/dot_general | solution.py:262
  39.7 0.1 slice.41
  39.8 0.1 multiply_convert_fusion.2
  39.9 0.2 copy.18
  40.1 0.5 copy.19.raw_ref
  40.6 68.2 %shard_map.140 = bf16[768,512]{1,0:T(8,128)(2,1)S(1)} custom-call(f32[768,512]{1,0:T(8,128)S(1)} %copy.19.raw_ref, f32[1,128]{1,0:T(1,128)S(1)} %bitcast.20, bf16[3,256,256]{2,1,0:T(8,128)(2,1)S(1)} %bitcast.19), custom_call_target="tpu_custom_call" | custom-call | tf_op jit(solution)/shard_map/pallas_call | solution.py:188
  108.8 0.1 pad_maximum_fusion.2
  108.9 0.8 collective-permute-start.2
  109.7 9.7 %collective-permute-done.2 = bf16[2,256,512]{2,1,0:T(8,128)(2,1)S(1)} collective-permute-done((bf16[2,256,512]{2,1,0:T(8,128)(2,1)S(1)}, bf16[2,256,512]{2,1,0:T(8,128)(2,1)S(1)}, u32[]{:S(2)}, u32[]{:S(2)}) %collective-permute-start.2) | collective-permute-done | bytes 524320 | tf_op jit(solution)/shard_map/ppermute | solution.py:279
  119.4 5.9 %fusion.14 = bf16[512,2048]{1,0:T(8,128)(2,1)} fusion(bf16[1024,4096]{1,0:T(8,128)(2,1)} %param.20, s32[]{:T(128)S(6)} %select_n.74, bf16[512,512]{1,0:T(8,128)(2,1)S(1)} %bitcast.26, bf16[512,512]{1,0:T(8,128)(2,1)S(1)} %bitcast.24, pred[]{:T(512)S(6)} %eq.10), kind=kOutput, calls=%fused_computation.18 | convolution fusion | flops 2153250816 | bytes 7340037 | tf_op jit(solution)/shard_map/dot_general | solution.py:284
  125.4 5.4 %collective-permute-start.3 = (bf16[512,2048]{1,0:T(8,128)(2,1)}, bf16[512,2048]{1,0:T(8,128)(2,1)S(1)}, u32[]{:S(2)}, u32[]{:S(2)}) collective-permute-start(bf16[512,2048]{1,0:T(8,128)(2,1)} %fusion.14), channel_id=1, source_target_pairs={{0,1},{1,0},{2,3},{3,2},{4,5},{5,4},{6,7},{7,6},{8,9},{9,8},{10,11... | collective-permute-start | bytes 6291464 | tf_op jit(solution)/shard_map/ppermute | solution.py:285
  130.8 0.1 broadcast_in_dim.35
  130.9 0.1 convert_element_type.71
  130.9 3.8 %collective-permute-done.3 = bf16[512,2048]{1,0:T(8,128)(2,1)S(1)} collective-permute-done((bf16[512,2048]{1,0:T(8,128)(2,1)}, bf16[512,2048]{1,0:T(8,128)(2,1)S(1)}, u32[]{:S(2)}, u32[]{:S(2)}) %collective-permute-start.3) | collective-permute-done | bytes 2097184 | tf_op jit(solution)/shard_map/ppermute | solution.py:285
  134.8 4.6 %convert_add_fusion = f32[512,2048]{1,0:T(8,128)S(1)} fusion(bf16[512,2048]{1,0:T(8,128)(2,1)S(1)} %collective-permute-done.3, bf16[1024,4096]{1,0:T(8,128)(2,1)} %param.20, s32[]{:T(128)S(6)} %select_n.73, bf16[512,512]{1,0:T(8,128)(2,1)S(1)} %bitcast.27, bf16[512,512]{1,0:T(8,128)(2,1)S(1)} %bitcast.25, pred[]{:T(512)S(6)} %eq.10), kind=kOutput, calls=%fused_computation.12 | convolution fusion | flops 2154299392 | bytes 11534341 | tf_op jit(solution)/shard_map/dot_general | solution.py:286
  139.4 1.1 slice.62
  140.5 1.1 fusion.18
  (32 shorter events, 0.3 us)
Async XLA Ops:
  0.6 26.1 %collective-permute-start = (bf16[256,2048]{1,0:T(8,128)(2,1)}, bf16[256,2048]{1,0:T(8,128)(2,1)S(1)}, u32[]{:S(2)}, u32[]{:S(2)}) collective-permute-start(bf16[256,2048]{1,0:T(8,128)(2,1)} %param.13), channel_id=1, source_target_pairs={{0,64},{64,0},{1,65},{65,1},{2,66},{66,2},{3,67},{67,3},{4,68},{68... | collective-permute-start | bytes 3145736 | tf_op jit(solution)/shard_map/ppermute | solution.py:242
  4.8 21.7 %collective-permute-start.1 = (s32[1,257]{1,0:T(1,128)S(1)}, s32[1,257]{1,0:T(1,128)S(1)}, u32[]{:S(2)}, u32[]{:S(2)}) collective-permute-start(s32[1,257]{1,0:T(1,128)S(1)} %pad_add_fusion), channel_id=1, source_target_pairs={{0,64},{64,0},{1,65},{65,1},{2,66},{66,2},{3,67},{67,3},{4,68},{68... | collective-permute-start | bytes 3092 | tf_op jit(solution)/shard_map/ppermute | solution.py:241
  7.0 4.6 %copy-start.2 = (bf16[4096,256]{1,0:T(8,128)(2,1)S(1)}, bf16[4096,256]{1,0:T(8,128)(2,1)}, u32[]{:S(2)}) copy-start(bf16[4096,256]{1,0:T(8,128)(2,1)} %param.19) | copy-start | bytes 6291460
  7.0 4.6 %copy-start.3 = (bf16[4096,256]{1,0:T(8,128)(2,1)S(1)}, bf16[4096,256]{1,0:T(8,128)(2,1)}, u32[]{:S(2)}) copy-start(bf16[4096,256]{1,0:T(8,128)(2,1)} %param.18) | copy-start | bytes 6291460
  11.6 1.2 copy-start.4
  11.6 1.2 copy-start.5
  11.6 14.9 %copy-start.7 = (s32[1,256]{1,0:T(1,128)S(1)}, s32[1,256]{1,0:T(1,128)}, u32[]{:S(2)}) copy-start(s32[1,256]{1,0:T(1,128)} %param.23) | copy-start | bytes 3076
  11.6 15.0 %copy-start.6 = (f32[4096]{0:T(1024)S(1)}, f32[4096]{0:T(1024)}, u32[]{:S(2)}) copy-start(f32[4096]{0:T(1024)} %param.16) | copy-start | bytes 49156
  11.6 15.1 %copy-start.1 = (bf16[256,2048]{1,0:T(8,128)(2,1)S(1)}, bf16[256,2048]{1,0:T(8,128)(2,1)}, u32[]{:S(2)}) copy-start(bf16[256,2048]{1,0:T(8,128)(2,1)} %param.13) | copy-start | bytes 3145732
  31.4 8.4 %copy-start.8 = (f32[128]{0:T(128)S(1)}, f32[128]{0:T(128)}, u32[]{:S(2)}) copy-start(f32[128]{0:T(128)} %param.22) | copy-start | bytes 1540
  39.7 0.9 copy-start
  108.9 10.5 %collective-permute-start.2 = (bf16[2,256,512]{2,1,0:T(8,128)(2,1)S(1)}, bf16[2,256,512]{2,1,0:T(8,128)(2,1)S(1)}, u32[]{:S(2)}, u32[]{:S(2)}) collective-permute-start(bf16[2,256,512]{2,1,0:T(8,128)(2,1)S(1)} %get-tuple-element.5), channel_id=1, source_target_pairs={{0,64},{64,0},{1,65},{65,1},{2,66},{66,2},{3,67},{67,3},{4,68},{68... | collective-permute-start | bytes 1572872 | tf_op jit(solution)/shard_map/ppermute | solution.py:279
  119.4 11.3 %copy-start.9 = (s32[1,4]{1,0:T(1,128)S(1)}, s32[1,4]{1,0:T(1,128)}, u32[]{:S(2)}) copy-start(s32[1,4]{1,0:T(1,128)} %param.24) | copy-start | bytes 52
  125.4 9.4 %collective-permute-start.3 = (bf16[512,2048]{1,0:T(8,128)(2,1)}, bf16[512,2048]{1,0:T(8,128)(2,1)S(1)}, u32[]{:S(2)}, u32[]{:S(2)}) collective-permute-start(bf16[512,2048]{1,0:T(8,128)(2,1)} %fusion.14), channel_id=1, source_target_pairs={{0,1},{1,0},{2,3},{3,2},{4,5},{5,4},{6,7},{7,6},{8,9},{9,8},{10,11... | collective-permute-start | bytes 6291464 | tf_op jit(solution)/shard_map/ppermute | solution.py:285

commit v4 on v3

--- a/solution.py
+++ b/solution.py
@@ -239,7 +239,15 @@
 
     notes = jnp.concatenate([masked, timesteps[:, None]], axis=1)
     other_notes = lax.ppermute(notes, "copy", SWAP)
-    other_tokens = lax.ppermute(clean_tokens, "copy", SWAP)
+    near_rows = lax.ppermute(
+        lax.dynamic_slice_in_dim(clean_tokens, core * (rows // 2), rows // 2, axis=0), "copy", SWAP
+    )
+    far_rows = lax.ppermute(near_rows, "tp", SWAP)
+    other_tokens = jnp.where(
+        core == 0,
+        jnp.concatenate([near_rows, far_rows], axis=0),
+        jnp.concatenate([far_rows, near_rows], axis=0),
+    )
     weights = jnp.concatenate(
         [
             lax.dynamic_slice_in_dim(w_query, mine * q_width, q_width, axis=1),
@@ -270,25 +278,28 @@
     spans = lax.axis_size("ctx")
     attended = attend(raw, q_gain[None, :], own, streams, rows, heads, spans)
     attended = attended.reshape(streams, rows, q_width)
-    kept = jnp.concatenate(
-        [attended[:1], lax.dynamic_slice_in_dim(attended, 1 + mine, 1, axis=0)], axis=0
-    )
-    given = jnp.concatenate(
-        [attended[:1], lax.dynamic_slice_in_dim(attended, 2 - mine, 1, axis=0)], axis=0
-    )
-    taken = lax.ppermute(given, "copy", SWAP)
-    head_rows = ordered(kept, taken, 2).reshape(2 * rows, 2 * q_width)
+    taken_clean = lax.ppermute(attended[0], "copy", SWAP)
+    taken_noised = lax.ppermute(
+        lax.dynamic_index_in_dim(attended, 2 - mine, axis=0, keepdims=False), "copy", SWAP
+    )
+    kept_noised = lax.dynamic_index_in_dim(attended, 1 + mine, axis=0, keepdims=False)
     half = w_out.shape[1] // 2
     away = lax.dynamic_slice_in_dim(w_out, (1 - core) * half, half, axis=1)
     here = lax.dynamic_slice_in_dim(w_out, core * half, half, axis=1)
-    sent = jnp.dot(head_rows, away, preferred_element_type=jnp.float32).astype(jnp.bfloat16)
-    received = lax.ppermute(sent, "tp", SWAP)
-    mixed = jnp.dot(head_rows, here, preferred_element_type=jnp.float32) + received.astype(
-        jnp.float32
-    )
-    clean_out = mixed[:rows].astype(jnp.bfloat16)
+
+    def partial(head_rows, weight):
+        return jnp.dot(head_rows, weight, preferred_element_type=jnp.float32)
+
+    clean_rows = ordered(attended[0], taken_clean, 1)
+    clean_sent = partial(clean_rows, away).astype(jnp.bfloat16)
+    clean_received = lax.ppermute(clean_sent, "tp", SWAP)
+    noised_rows = ordered(kept_noised, taken_noised, 1)
+    noised_sent = partial(noised_rows, away).astype(jnp.bfloat16)
+    noised_received = lax.ppermute(noised_sent, "tp", SWAP)
+    clean_out = (partial(clean_rows, here) + clean_received.astype(jnp.float32)).astype(jnp.bfloat16)
+    mixed = partial(noised_rows, here) + noised_received.astype(jnp.float32)
     live_rows = jnp.repeat(block_live, BLK, axis=1).astype(jnp.float32)
-    noised_out = (mixed[None, rows:] * live_rows[:, :, None]).astype(jnp.bfloat16)
+    noised_out = (mixed[None] * live_rows[:, :, None]).astype(jnp.bfloat16)
     return (clean_out, noised_out)
 
 

time: 142 us -> 141 us (level)
  waiting for transfers between devices: 27.3 us -> 8.12 us
  matrix products: 18.7 us -> 25.9 us
  starting transfers between devices: 9.23 us -> 15.4 us
  Pallas kernels: 68.2 us -> 71.5 us
  local copies, waits for them, and re-layouts: 7.84 us -> 11 us
  other arithmetic: 8.24 us -> 6.55 us
    ppermute x1, waiting for transfers between devices: 13.7 us -> 3.03 us  [on_device(): other_notes = lax.ppermute(notes, 'copy', SWAP)]
    ppermute x3 -> x6, waiting for transfers between devices: 13.6 us -> 5.09 us  [the longest x1 3.64 us: on_device(): taken_clean = lax.ppermute(attended[0], 'copy', SWAP)]
    dot_general x2 -> x4, matrix products: 10.5 us -> 17.8 us  [partial(): return jnp.dot(head_rows, weight, preferred_element_type=jnp.float32)]
    ppermute x3 -> x6, starting transfers between devices: 9 us -> 15.2 us  [the longest x1 7.55 us: on_device(): clean_received = lax.ppermute(clean_sent, 'tp', SWAP)]
    pallas_call x1, Pallas kernels: 68.2 us -> 71.5 us  [attend(): pl.pallas_call(functools.partial(attend_kernel, rows, heads, streams, spa...]
    unnamed x21 -> x25, local copies, waits for them, and re-layouts: 0.52 us -> 2.63 us
  transfers between devices with their start and end apart: 4 -> 7, of which waited for: 3 -> 3; matrix products, arithmetic and copies ran while one was open for 6% -> 15% of each run, Pallas kernels for 0% -> 0%
where the time goes in v4:
time: 141 us
  Pallas kernels  71.5 us (51%)
  matrix products  25.9 us (18%)
  starting transfers between devices  15.4 us (11%)
  local copies, waits for them, and re-layouts  11 us (8%)
  waiting for transfers between devices  8.12 us (6%)
  other arithmetic  6.55 us (5%)
  between operations  2.13 us (2%)
    pallas_call x1, Pallas kernels, attend(): pl.pallas_call(functools.partial(attend_kernel, rows, heads, streams, spa...  71.5 us
    dot_general x4, matrix products, partial(): return jnp.dot(head_rows, weight, preferred_element_type=jnp.float32)  17.8 us
    dot_general x1, matrix products, on_device(): jnp.dot(all_rows.reshape(streams * rows, -1), weights, preferred_element_...  8.17 us
    ppermute x1, starting transfers between devices, on_device(): clean_received = lax.ppermute(clean_sent, 'tp', SWAP)  7.55 us
    dynamic_slice x1, local copies, waits for them, and re-layouts, on_device(): lax.dynamic_slice_in_dim(w_query, mine * q_width, q_width, axis=1)  4.57 us
    ppermute x1, waiting for transfers between devices, on_device(): taken_clean = lax.ppermute(attended[0], 'copy', SWAP)  3.64 us
    ppermute x1, waiting for transfers between devices, on_device(): other_notes = lax.ppermute(notes, 'copy', SWAP)  3.03 us
    ppermute x1, starting transfers between devices, on_device(): lax.ppermute(lax.dynamic_slice_in_dim(clean_tokens, core * (rows // 2), r...  2.82 us
  transfers between devices with their start and end apart: 7, of which 3 were waited for; matrix products, arithmetic and copies ran while one was open for 15% of the time, Pallas kernels for 0%

profile of v4, /device:TPU:121, one launch (start us, length us, event | category | flops | bytes accessed | tf_op | source)
XLA Modules:
  0.0 140.7 jit_solution(7030414927075110903)
XLA Ops:
  0.6 1.1 constant_dynamic-slice_fusion.3
  1.7 2.8 %collective-permute-start = (bf16[128,2048]{1,0:T(8,128)(2,1)S(1)}, bf16[128,2048]{1,0:T(8,128)(2,1)S(1)}, u32[]{:S(2)}, u32[]{:S(2)}) collective-permute-start(bf16[128,2048]{1,0:T(8,128)(2,1)S(1)} %constant_dynamic-slice_fusion.3), channel_id=1, source_target_pairs={{0,64},{64,0},{1,65},{65,1},{2,66},{66,2},{3,67},{67,3},{4,68},{68... | collective-permute-start | bytes 1572872 | tf_op jit(solution)/shard_map/ppermute | solution.py:242
  5.2 0.7 pad_add_fusion
  5.9 0.2 collective-permute-start.2
  6.1 4.6 %constant_dynamic-slice_fusion.2 = bf16[4096,512]{1,0:T(8,128)(2,1)} fusion(bf16[4096,1024]{1,0:T(8,128)(2,1)} %param.17, s32[]{:T(128)S(6)} %select_n.95), kind=kLoop, calls=%fused_computation.54 | loop fusion | bytes 8388612 | tf_op jit(solution)/shard_map/dynamic_slice | solution.py:253
  10.7 1.1 constant_dynamic-slice_fusion
  11.9 0.6 fusion.40
  13.1 3.0 %collective-permute-done.2 = s32[1,257]{1,0:T(1,128)S(1)} collective-permute-done((s32[1,257]{1,0:T(1,128)S(1)}, s32[1,257]{1,0:T(1,128)S(1)}, u32[]{:S(2)}, u32[]{:S(2)}) %collective-permute-start.2) | collective-permute-done | bytes 1060 | tf_op jit(solution)/shard_map/ppermute | solution.py:241
  16.1 0.1 fusion.47
  16.3 1.7 %collective-permute-start.1 = (bf16[128,2048]{1,0:T(8,128)(2,1)S(1)}, bf16[128,2048]{1,0:T(8,128)(2,1)S(1)}, u32[]{:S(2)}, u32[]{:S(2)}) collective-permute-start(bf16[128,2048]{1,0:T(8,128)(2,1)S(1)} %collective-permute-done), channel_id=1, source_target_pairs={{0,1},{1,0},{2,3},{3,2},{4,5},{5,4},{6,7},{7,6},{8,9},{9,8},{10,11... | collective-permute-start | bytes 1572872 | tf_op jit(solution)/shard_map/ppermute | solution.py:245
  18.0 1.4 %collective-permute-done.1 = bf16[128,2048]{1,0:T(8,128)(2,1)S(1)} collective-permute-done((bf16[128,2048]{1,0:T(8,128)(2,1)S(1)}, bf16[128,2048]{1,0:T(8,128)(2,1)S(1)}, u32[]{:S(2)}, u32[]{:S(2)}) %collective-permute-start.1) | collective-permute-done | bytes 524320 | tf_op jit(solution)/shard_map/ppermute | solution.py:245
  19.5 0.2 maximum_select_fusion.2
  19.7 0.6 fusion.6
  20.4 0.8 fusion.7
  21.2 0.9 multiply_convert_fusion.1
  22.1 1.7 %multiply_convert_fusion = bf16[2,256,4096]{2,1,0:T(8,128)(2,1)S(1)} fusion(f32[2,4096]{1,0:T(2,128)S(1)} %multiply_add_fusion, f32[256,4096]{1,0:T(8,128)S(1)} %fusion.7, f32[4096]{0:T(1024)S(1)} %fusion.41, pred[2,256]{1,0:T(4,128)(4,1)S(1)} %slice_compare_fusion), kind=kLoop, calls=%fused_computation | loop fusion | flops 6291456 | bytes 8438272 | tf_op jit(solution)/shard_map/convert.2
  23.8 0.5 pad_maximum_fusion
  24.4 8.2 %fusion = f32[768,768]{0,1:T(8,128)S(1)} fusion(bf16[768,4096]{1,0:T(8,128)(2,1)S(1)} %bitcast.23, bf16[4096,128]{1,0:T(8,128)(2,1)S(1)} %get-tuple-element.4, bf16[4096,128]{1,0:T(8,128)(2,1)} %get-tuple-element.5, bf16[4096,512]{1,0:T(8,128)(2,1)} %constant_dynamic-slice_fusion.2), kind=kOutput, calls=%fused_computation.2 | convolution fusion | flops 4850712576 | bytes 14942208 | tf_op jit(solution)/shard_map/dot_general | solution.py:270
  32.7 1.2 slice.29
  33.9 0.1 multiply_convert_fusion.2
  34.0 0.2 copy.18
  34.2 1.9 %copy.19.raw_ref = f32[768,512]{1,0:T(8,128)S(1)} copy(f32[768,512]{0,1:T(8,128)} %slice.29) | data formatting | bytes 3145728
  36.1 71.5 %shard_map.140 = bf16[768,512]{1,0:T(8,128)(2,1)S(1)} custom-call(f32[768,512]{1,0:T(8,128)S(1)} %copy.19.raw_ref, f32[1,128]{1,0:T(1,128)S(1)} %bitcast.20, bf16[3,256,256]{2,1,0:T(8,128)(2,1)S(1)} %bitcast.19), custom_call_target="tpu_custom_call" | custom-call | tf_op jit(solution)/shard_map/pallas_call | solution.py:188
  107.6 2.7 %collective-permute-start.3 = (bf16[256,512]{1,0:T(8,128)(2,1)S(1)}, bf16[256,512]{1,0:T(8,128)(2,1)S(1)}, u32[]{:S(2)}, u32[]{:S(2)}) collective-permute-start(bf16[256,512]{1,0:T(8,128)(2,1)S(1)} %slice.26), channel_id=1, source_target_pairs={{0,64},{64,0},{1,65},{65,1},{2,66},{66,2},{3,67},{67,3},{4,68},{68... | collective-permute-start | bytes 786440 | tf_op jit(solution)/shard_map/ppermute | solution.py:281
  110.3 0.4 collective-permute-start.5
  110.8 3.6 %collective-permute-done.3 = bf16[256,512]{1,0:T(8,128)(2,1)S(1)} collective-permute-done((bf16[256,512]{1,0:T(8,128)(2,1)S(1)}, bf16[256,512]{1,0:T(8,128)(2,1)S(1)}, u32[]{:S(2)}, u32[]{:S(2)}) %collective-permute-start.3) | collective-permute-done | bytes 262176 | tf_op jit(solution)/shard_map/ppermute | solution.py:281
  114.4 0.7 copy-done.9
  115.1 4.4 %fusion.28 = bf16[256,2048]{1,0:T(8,128)(2,1)} fusion(bf16[1024,4096]{1,0:T(8,128)(2,1)} %param.20, s32[]{:T(128)S(6)} %select_n.99, bf16[256,512]{1,0:T(8,128)(2,1)S(1)} %collective-permute-done.3, bf16[256,512]{1,0:T(8,128)(2,1)S(1)} %slice.26, pred[]{:T(512)S(6)} %eq.13), kind=kOutput, calls=%fused_computation.25 | convolution fusion | flops 1076625408 | bytes 5767173 | tf_op jit(solution)/shard_map/dot_general | solution.py:291
  119.5 7.5 %collective-permute-start.4 = (bf16[256,2048]{1,0:T(8,128)(2,1)}, bf16[256,2048]{1,0:T(8,128)(2,1)S(1)}, u32[]{:S(2)}, u32[]{:S(2)}) collective-permute-start(bf16[256,2048]{1,0:T(8,128)(2,1)} %fusion.28), channel_id=1, source_target_pairs={{0,1},{1,0},{2,3},{3,2},{4,5},{5,4},{6,7},{7,6},{8,9},{9,8},{10,11... | collective-permute-start | bytes 3145736 | tf_op jit(solution)/shard_map/ppermute | solution.py:295
  127.1 4.4 %fusion.31 = bf16[256,2048]{1,0:T(8,128)(2,1)} fusion(bf16[1024,4096]{1,0:T(8,128)(2,1)} %param.20, s32[]{:T(128)S(6)} %select_n.99, bf16[256,512]{1,0:T(8,128)(2,1)S(1)} %collective-permute-done.5, bf16[256,512]{1,0:T(8,128)(2,1)S(1)} %get-tuple-element.2, pred[]{:T(512)S(6)} %eq.13), kind=kOutput, calls=%fused_computation.26 | convolution fusion | flops 1076625408 | bytes 5767173 | tf_op jit(solution)/shard_map/dot_general | solution.py:291
  131.7 4.4 %fusion.25 = bf16[256,2048]{1,0:T(8,128)(2,1)} fusion(bf16[1024,4096]{1,0:T(8,128)(2,1)} %param.20, s32[]{:T(128)S(6)} %select_n.98, bf16[256,2048]{1,0:T(8,128)(2,1)S(1)} %collective-permute-done.4, bf16[256,512]{1,0:T(8,128)(2,1)S(1)} %copy-done.10, bf16[256,512]{1,0:T(8,128)(2,1)S(1)} %slice.26, pred[]{:T(512)S(6)} %eq.13), kind=kOutput, calls=%fused_computation.24 | convolution fusion | flops 1077673984 | bytes 6815749 | tf_op jit(solution)/shard_map/dot_general | solution.py:291
  136.2 4.5 %fusion.37 = bf16[1,256,2048]{2,1,0:T(8,128)(2,1)} fusion(bf16[1024,4096]{1,0:T(8,128)(2,1)} %param.20, s32[]{:T(128)S(6)} %select_n.98, bf16[256,2048]{1,0:T(8,128)(2,1)S(1)} %collective-permute-done.6, f32[256]{0:T(256)S(1)} %convert_element_type.82, bf16[256,512]{1,0:T(8,128)(2,1)S(1)} %collective-permute-done.5, ...), kind=kOutput, calls=%fused_computation.28 | convolution fusion | flops 1078198272 | bytes 6816773 | tf_op jit(solution)/shard_map/dot_general | solution.py:291
  (43 shorter events, 0.5 us)
Async XLA Ops:
  1.7 14.5 %collective-permute-start = (bf16[128,2048]{1,0:T(8,128)(2,1)S(1)}, bf16[128,2048]{1,0:T(8,128)(2,1)S(1)}, u32[]{:S(2)}, u32[]{:S(2)}) collective-permute-start(bf16[128,2048]{1,0:T(8,128)(2,1)S(1)} %constant_dynamic-slice_fusion.3), channel_id=1, source_target_pairs={{0,64},{64,0},{1,65},{65,1},{2,66},{66,2},{3,67},{67,3},{4,68},{68... | collective-permute-start | bytes 1572872 | tf_op jit(solution)/shard_map/ppermute | solution.py:242
  5.9 10.2 %collective-permute-start.2 = (s32[1,257]{1,0:T(1,128)S(1)}, s32[1,257]{1,0:T(1,128)S(1)}, u32[]{:S(2)}, u32[]{:S(2)}) collective-permute-start(s32[1,257]{1,0:T(1,128)S(1)} %pad_add_fusion), channel_id=1, source_target_pairs={{0,64},{64,0},{1,65},{65,1},{2,66},{66,2},{3,67},{67,3},{4,68},{68... | collective-permute-start | bytes 3092 | tf_op jit(solution)/shard_map/ppermute | solution.py:241
  6.1 4.6 %copy-start.2 = (bf16[4096,256]{1,0:T(8,128)(2,1)S(1)}, bf16[4096,256]{1,0:T(8,128)(2,1)}, u32[]{:S(2)}) copy-start(bf16[4096,256]{1,0:T(8,128)(2,1)} %param.19) | copy-start | bytes 6291460
  6.1 4.6 %copy-start.3 = (bf16[4096,256]{1,0:T(8,128)(2,1)S(1)}, bf16[4096,256]{1,0:T(8,128)(2,1)}, u32[]{:S(2)}) copy-start(bf16[4096,256]{1,0:T(8,128)(2,1)} %param.18) | copy-start | bytes 6291460
  10.7 1.2 copy-start.5
  10.7 2.4 %copy-start.4 = (bf16[4096]{0:T(1024)(128)(2,1)S(1)}, bf16[4096]{0:T(1024)(128)(2,1)}, u32[]{:S(2)}) copy-start(bf16[4096]{0:T(1024)(128)(2,1)} %param.14) | copy-start | bytes 24580
  10.7 5.4 %copy-start.7 = (s32[1,256]{1,0:T(1,128)S(1)}, s32[1,256]{1,0:T(1,128)}, u32[]{:S(2)}) copy-start(s32[1,256]{1,0:T(1,128)} %param.23) | copy-start | bytes 3076
  10.7 7.2 %copy-start.6 = (f32[4096]{0:T(1024)S(1)}, f32[4096]{0:T(1024)}, u32[]{:S(2)}) copy-start(f32[4096]{0:T(1024)} %param.16) | copy-start | bytes 49156
  10.7 9.0 %copy-start.1 = (bf16[256,2048]{1,0:T(8,128)(2,1)S(1)}, bf16[256,2048]{1,0:T(8,128)(2,1)}, u32[]{:S(2)}) copy-start(bf16[256,2048]{1,0:T(8,128)(2,1)} %param.13) | copy-start | bytes 3145732
  16.3 3.2 %collective-permute-start.1 = (bf16[128,2048]{1,0:T(8,128)(2,1)S(1)}, bf16[128,2048]{1,0:T(8,128)(2,1)S(1)}, u32[]{:S(2)}, u32[]{:S(2)}) collective-permute-start(bf16[128,2048]{1,0:T(8,128)(2,1)S(1)} %collective-permute-done), channel_id=1, source_target_pairs={{0,1},{1,0},{2,3},{3,2},{4,5},{5,4},{6,7},{7,6},{8,9},{9,8},{10,11... | collective-permute-start | bytes 1572872 | tf_op jit(solution)/shard_map/ppermute | solution.py:245
  24.4 9.5 %copy-start.8 = (f32[128]{0:T(128)S(1)}, f32[128]{0:T(128)}, u32[]{:S(2)}) copy-start(f32[128]{0:T(128)} %param.22) | copy-start | bytes 1540
  32.6 3.5 %copy-start = (f32[128]{0:T(128)S(1)}, f32[128]{0:T(128)}, u32[]{:S(2)}) copy-start(f32[128]{0:T(128)} %param.21) | copy-start | bytes 1540
  107.6 6.8 %collective-permute-start.3 = (bf16[256,512]{1,0:T(8,128)(2,1)S(1)}, bf16[256,512]{1,0:T(8,128)(2,1)S(1)}, u32[]{:S(2)}, u32[]{:S(2)}) collective-permute-start(bf16[256,512]{1,0:T(8,128)(2,1)S(1)} %slice.26), channel_id=1, source_target_pairs={{0,64},{64,0},{1,65},{65,1},{2,66},{66,2},{3,67},{67,3},{4,68},{68... | collective-permute-start | bytes 786440 | tf_op jit(solution)/shard_map/ppermute | solution.py:281
  110.3 16.7 %collective-permute-start.5 = (bf16[256,512]{1,0:T(8,128)(2,1)S(1)}, bf16[256,512]{1,0:T(8,128)(2,1)S(1)}, u32[]{:S(2)}, u32[]{:S(2)}) collective-permute-start(bf16[256,512]{1,0:T(8,128)(2,1)S(1)} %get-tuple-element.3), channel_id=1, source_target_pairs={{0,64},{64,0},{1,65},{65,1},{2,66},{66,2},{3,67},{67,3},{4,68},{68... | collective-permute-start | bytes 786440 | tf_op jit(solution)/shard_map/ppermute | solution.py:282
  114.4 0.7 copy-start.9
  119.5 12.0 %copy-start.11 = (s32[1,4]{1,0:T(1,128)S(1)}, s32[1,4]{1,0:T(1,128)}, u32[]{:S(2)}) copy-start(s32[1,4]{1,0:T(1,128)} %param.24) | copy-start | bytes 52
  119.5 12.2 %copy-start.10 = (bf16[256,512]{1,0:T(8,128)(2,1)S(1)}, bf16[256,512]{1,0:T(8,128)(2,1)}, u32[]{:S(2)}) copy-start(bf16[256,512]{1,0:T(8,128)(2,1)} %copy-done.9) | copy-start | bytes 786436
  119.5 12.2 %collective-permute-start.4 = (bf16[256,2048]{1,0:T(8,128)(2,1)}, bf16[256,2048]{1,0:T(8,128)(2,1)S(1)}, u32[]{:S(2)}, u32[]{:S(2)}) collective-permute-start(bf16[256,2048]{1,0:T(8,128)(2,1)} %fusion.28), channel_id=1, source_target_pairs={{0,1},{1,0},{2,3},{3,2},{4,5},{5,4},{6,7},{7,6},{8,9},{9,8},{10,11... | collective-permute-start | bytes 3145736 | tf_op jit(solution)/shard_map/ppermute | solution.py:295
  131.5 4.7 %collective-permute-start.6 = (bf16[256,2048]{1,0:T(8,128)(2,1)}, bf16[256,2048]{1,0:T(8,128)(2,1)S(1)}, u32[]{:S(2)}, u32[]{:S(2)}) collective-permute-start(bf16[256,2048]{1,0:T(8,128)(2,1)} %fusion.31), channel_id=1, source_target_pairs={{0,1},{1,0},{2,3},{3,2},{4,5},{5,4},{6,7},{7,6},{8,9},{9,8},{10,11... | collective-permute-start | bytes 3145736 | tf_op jit(solution)/shard_map/ppermute | solution.py:298

commit v5 on v4

--- a/solution.py
+++ b/solution.py
@@ -202,6 +202,121 @@
             vmem_limit_bytes=48 * 2**20, collective_id=0, has_side_effects=True
         ),
     )(raw, q_gain, own)
+
+
+def project_kernel(
+    rows, att_ref, w_out_ref, live_ref, clean_ref, noised_ref,
+    weight_ref, taken_ref, away_ref, here_ref, sent_ref, got_ref, give_sem, take_sem, send_sem, recv_sem, load_sem,
+):
+    mine = lax.axis_index("copy")
+    core = lax.axis_index("tp")
+    depth = att_ref.shape[1]
+    loads = []
+    for number, owner in enumerate((mine, 1 - mine)):
+        at = pl.ds(pl.multiple_of(owner * depth, depth), depth)
+        load = pltpu.make_async_copy(w_out_ref.at[at], weight_ref.at[at], load_sem.at[number])
+        load.start()
+        loads.append(load)
+    barrier = pltpu.get_barrier_semaphore()
+    pl.semaphore_signal(barrier, inc=1, device_id={"copy": 1 - mine}, device_id_type=MESH)
+    pl.semaphore_signal(barrier, inc=1, device_id={"tp": 1 - core}, device_id_type=MESH)
+    pl.semaphore_wait(barrier, 2)
+
+    pieces, _, width = sent_ref.shape
+
+    def part(start):
+        return pl.ds(pl.multiple_of(start, rows), rows)
+
+    gifts = [
+        pltpu.make_async_remote_copy(
+            src_ref=att_ref.at[part(start)],
+            dst_ref=taken_ref.at[pl.ds(number * rows, rows)],
+            send_sem=give_sem.at[number],
+            recv_sem=take_sem.at[number],
+            device_id={"copy": 1 - mine},
+            device_id_type=MESH,
+        )
+        for number, start in enumerate((0, (2 - mine) * rows))
+    ]
+    for gift in gifts:
+        gift.start()
+
+    def weight(half, owner, piece):
+        return weight_ref[
+            pl.ds(pl.multiple_of(owner * depth, depth), depth),
+            pl.ds(pl.multiple_of((half * pieces + piece) * width, width), width),
+        ]
+
+    def product(values, half, owner, piece):
+        return jnp.dot(values, weight(half, owner, piece), preferred_element_type=jnp.float32)
+
+    kept = jnp.concatenate([att_ref[:rows], att_ref[part((1 + mine) * rows)]], axis=0)
+    loads[0].wait()
+    for piece in range(pieces):
+        away_ref[piece] = product(kept, 1 - core, mine, piece)
+    for piece in range(pieces):
+        here_ref[piece] = product(kept, core, mine, piece)
+    for gift in gifts:
+        gift.wait_recv()
+    loads[1].wait()
+    taken = taken_ref[...]
+    copies = []
+    for piece in range(pieces):
+        sent_ref[piece] = (away_ref[piece] + product(taken, 1 - core, 1 - mine, piece)).astype(jnp.bfloat16)
+        copy = pltpu.make_async_remote_copy(
+            src_ref=sent_ref.at[piece],
+            dst_ref=got_ref.at[piece],
+            send_sem=send_sem.at[piece],
+            recv_sem=recv_sem.at[piece],
+            device_id={"tp": 1 - core},
+            device_id_type=MESH,
+        )
+        copy.start()
+        copies.append(copy)
+    for piece in range(pieces):
+        here_ref[piece] += product(taken, core, 1 - mine, piece)
+    for piece, copy in enumerate(copies):
+        copy.wait_recv()
+        total = here_ref[piece] + got_ref[piece].astype(jnp.float32)
+        at = pl.ds(piece * width, width)
+        clean_ref[:, at] = total[:rows].astype(jnp.bfloat16)
+        noised_ref[:, at] = (total[rows:] * live_ref[...]).astype(jnp.bfloat16)
+    for copy in gifts + copies:
+        copy.wait_send()
+
+
+def project(attended, w_out, live_rows):
+    rows = live_rows.shape[0]
+    half = w_out.shape[1] // 2
+    pieces = 4
+    width = half // pieces
+    out = jax.ShapeDtypeStruct((rows, half), jnp.bfloat16)
+    return pl.pallas_call(
+        functools.partial(project_kernel, rows),
+        out_shape=(out, out),
+        in_specs=[
+            pl.BlockSpec(memory_space=pltpu.VMEM),
+            pl.BlockSpec(memory_space=pltpu.HBM),
+            pl.BlockSpec(memory_space=pltpu.VMEM),
+        ],
+        out_specs=(pl.BlockSpec(memory_space=pltpu.VMEM),) * 2,
+        scratch_shapes=[
+            pltpu.VMEM(w_out.shape, jnp.bfloat16),
+            pltpu.VMEM((2 * rows, attended.shape[1]), jnp.bfloat16),
+            pltpu.VMEM((pieces, 2 * rows, width), jnp.float32),
+            pltpu.VMEM((pieces, 2 * rows, width), jnp.float32),
+            pltpu.VMEM((pieces, 2 * rows, width), jnp.bfloat16),
+            pltpu.VMEM((pieces, 2 * rows, width), jnp.bfloat16),
+            pltpu.SemaphoreType.DMA((2,)),
+            pltpu.SemaphoreType.DMA((2,)),
+            pltpu.SemaphoreType.DMA((pieces,)),
+            pltpu.SemaphoreType.DMA((pieces,)),
+            pltpu.SemaphoreType.DMA((2,)),
+        ],
+        compiler_params=pltpu.CompilerParams(
+            vmem_limit_bytes=44 * 2**20, collective_id=1, has_side_effects=True
+        ),
+    )(attended, w_out, live_rows)
 
 
 SWAP = [(0, 1), (1, 0)]
@@ -277,29 +392,9 @@
     own = jnp.concatenate([keys, values], axis=1).reshape(streams, rows, 2 * HD)
     spans = lax.axis_size("ctx")
     attended = attend(raw, q_gain[None, :], own, streams, rows, heads, spans)
-    attended = attended.reshape(streams, rows, q_width)
-    taken_clean = lax.ppermute(attended[0], "copy", SWAP)
-    taken_noised = lax.ppermute(
-        lax.dynamic_index_in_dim(attended, 2 - mine, axis=0, keepdims=False), "copy", SWAP
-    )
-    kept_noised = lax.dynamic_index_in_dim(attended, 1 + mine, axis=0, keepdims=False)
-    half = w_out.shape[1] // 2
-    away = lax.dynamic_slice_in_dim(w_out, (1 - core) * half, half, axis=1)
-    here = lax.dynamic_slice_in_dim(w_out, core * half, half, axis=1)
-
-    def partial(head_rows, weight):
-        return jnp.dot(head_rows, weight, preferred_element_type=jnp.float32)
-
-    clean_rows = ordered(attended[0], taken_clean, 1)
-    clean_sent = partial(clean_rows, away).astype(jnp.bfloat16)
-    clean_received = lax.ppermute(clean_sent, "tp", SWAP)
-    noised_rows = ordered(kept_noised, taken_noised, 1)
-    noised_sent = partial(noised_rows, away).astype(jnp.bfloat16)
-    noised_received = lax.ppermute(noised_sent, "tp", SWAP)
-    clean_out = (partial(clean_rows, here) + clean_received.astype(jnp.float32)).astype(jnp.bfloat16)
-    mixed = partial(noised_rows, here) + noised_received.astype(jnp.float32)
-    live_rows = jnp.repeat(block_live, BLK, axis=1).astype(jnp.float32)
-    noised_out = (mixed[None] * live_rows[:, :, None]).astype(jnp.bfloat16)
+    live_rows = jnp.repeat(block_live[0], BLK)[:, None].astype(jnp.float32)
+    clean_out, noised_out = project(attended, w_out, live_rows)
+    noised_out = noised_out[None]
     return (clean_out, noised_out)
 
 

time: 141 us -> 142 us (level)
  Pallas kernels: 71.5 us -> 98.1 us
  matrix products: 25.9 us -> 8.4 us
  starting transfers between devices: 15.4 us -> 4.7 us
  other arithmetic: 6.55 us -> 11.5 us
  waiting for transfers between devices: 8.12 us -> 3.33 us
  local copies, waits for them, and re-layouts: 11 us -> 13.4 us
    pallas_call x0 -> x1, Pallas kernels: none -> 26.3 us  [project(): pl.pallas_call(functools.partial(project_kernel, rows), out_shape=(out, o...]
    dot_general x4 -> x0, matrix products: 17.8 us -> none  [partial(): return jnp.dot(head_rows, weight, preferred_element_type=jnp.float32)]
    ppermute x4 -> x0, starting transfers between devices: 10.7 us -> none  [the longest x1 7.55 us: on_device(): clean_received = lax.ppermute(clean_sent, 'tp', SWAP)]
    ppermute x4 -> x0, waiting for transfers between devices: 3.65 us -> none  [the longest x1 3.64 us: on_device(): taken_clean = lax.ppermute(attended[0], 'copy', SWAP)]
    concatenate x1, other arithmetic: 0.54 us -> 3.74 us  [on_device(): all_rows = jnp.concatenate([base[None], noisy], axis=0).astype(jnp.bfloat16)]
    unnamed x25 -> x29, local copies, waits for them, and re-layouts: 2.63 us -> 4.88 us
  transfers between devices with their start and end apart: 7 -> 3, of which waited for: 3 -> 2; matrix products, arithmetic and copies ran while one was open for 15% -> 6% of each run, Pallas kernels for 0% -> 0%
where the time goes in v5:
time: 142 us
  Pallas kernels  98.1 us (69%)
  local copies, waits for them, and re-layouts  13.4 us (9%)
  other arithmetic  11.5 us (8%)
  matrix products  8.4 us (6%)
  starting transfers between devices  4.7 us (3%)
  waiting for transfers between devices  3.33 us (2%)
  between operations  2.25 us (2%)
    pallas_call x1, Pallas kernels, attend(): pl.pallas_call(functools.partial(attend_kernel, rows, heads, streams, spa...  71.7 us
    pallas_call x1, Pallas kernels, project(): pl.pallas_call(functools.partial(project_kernel, rows), out_shape=(out, o...  26.3 us
    dot_general x1, matrix products, on_device(): jnp.dot(all_rows.reshape(streams * rows, -1), weights, preferred_element_...  8.4 us
    unnamed x29, local copies, waits for them, and re-layouts  4.88 us
    dynamic_slice x1, local copies, waits for them, and re-layouts, on_device(): lax.dynamic_slice_in_dim(w_query, mine * q_width, q_width, axis=1)  4.65 us
    concatenate x1, other arithmetic, on_device(): all_rows = jnp.concatenate([base[None], noisy], axis=0).astype(jnp.bfloat16)  3.74 us
    another operation x2, other arithmetic  3.62 us
  transfers between devices with their start and end apart: 3, of which 2 were waited for; matrix products, arithmetic and copies ran while one was open for 6% of the time, Pallas kernels for 0%

profile of v5, /device:TPU:121, one launch (start us, length us, event | category | flops | bytes accessed | tf_op | source)
XLA Modules:
  0.0 141.6 jit_solution(7286944189272959095)
XLA Ops:
  0.6 1.1 constant_dynamic-slice_fusion.3
  1.7 2.8 %collective-permute-start = (bf16[128,2048]{1,0:T(8,128)(2,1)S(1)}, bf16[128,2048]{1,0:T(8,128)(2,1)S(1)}, u32[]{:S(2)}, u32[]{:S(2)}) collective-permute-start(bf16[128,2048]{1,0:T(8,128)(2,1)S(1)} %constant_dynamic-slice_fusion.3), channel_id=1, source_target_pairs={{0,64},{64,0},{1,65},{65,1},{2,66},{66,2},{3,67},{67,3},{4,68},{68... | collective-permute-start | bytes 1572872 | tf_op jit(solution)/shard_map/ppermute | solution.py:357
  5.2 0.7 pad_add_fusion
  5.9 0.2 collective-permute-start.2
  6.1 1.3 fusion.8
  8.1 0.0 copy-start.5
  8.1 4.6 %constant_dynamic-slice_fusion.2 = bf16[4096,512]{1,0:T(8,128)(2,1)} fusion(bf16[4096,1024]{1,0:T(8,128)(2,1)} %param.17, s32[]{:T(128)S(6)} %select_n.69), kind=kLoop, calls=%fused_computation.35 | loop fusion | bytes 8388612 | tf_op jit(solution)/shard_map/dynamic_slice | solution.py:368
  12.8 1.1 constant_dynamic-slice_fusion
  14.0 0.1 broadcast_in_dim.54
  14.1 0.1 convert_element_type.48.live_ref
  14.2 1.9 %collective-permute-done.2 = s32[1,257]{1,0:T(1,128)S(1)} collective-permute-done((s32[1,257]{1,0:T(1,128)S(1)}, s32[1,257]{1,0:T(1,128)S(1)}, u32[]{:S(2)}, u32[]{:S(2)}) %collective-permute-start.2) | collective-permute-done | bytes 1060 | tf_op jit(solution)/shard_map/ppermute | solution.py:356
  16.1 0.1 fusion.11
  16.3 1.7 %collective-permute-start.1 = (bf16[128,2048]{1,0:T(8,128)(2,1)S(1)}, bf16[128,2048]{1,0:T(8,128)(2,1)S(1)}, u32[]{:S(2)}, u32[]{:S(2)}) collective-permute-start(bf16[128,2048]{1,0:T(8,128)(2,1)S(1)} %collective-permute-done), channel_id=1, source_target_pairs={{0,1},{1,0},{2,3},{3,2},{4,5},{5,4},{6,7},{7,6},{8,9},{9,8},{10,11... | collective-permute-start | bytes 1572872 | tf_op jit(solution)/shard_map/ppermute | solution.py:360
  17.9 0.1 multiply_add_fusion
  18.0 1.4 %collective-permute-done.1 = bf16[128,2048]{1,0:T(8,128)(2,1)S(1)} collective-permute-done((bf16[128,2048]{1,0:T(8,128)(2,1)S(1)}, bf16[128,2048]{1,0:T(8,128)(2,1)S(1)}, u32[]{:S(2)}, u32[]{:S(2)}) %collective-permute-start.1) | collective-permute-done | bytes 524320 | tf_op jit(solution)/shard_map/ppermute | solution.py:360
  19.5 0.2 maximum_select_fusion.2
  19.7 0.6 fusion.6
  20.4 0.8 fusion.7
  21.2 1.9 %multiply_convert_fusion.1 = bf16[1,256,4096]{2,1,0:T(8,128)(2,1)} fusion(bf16[1,256,2048]{2,1,0:T(8,128)(2,1)S(1)} %bitcast.15, bf16[1,256,2048]{2,1,0:T(8,128)(2,1)S(1)} %bitcast.16, f32[4096]{0:T(1024)S(1)} %convert_element_type.40, f32[256]{0:T(256)S(1)} %add_rsqrt_fusion.1, pred[]{:T(512)S(6)} %eq.13), kind=kLoop, calls=%fused_computation.12 | loop fusion | flops 13631488 | bytes 4211713 | tf_op jit(solution)/shard_map/convert.1
  23.2 1.7 %multiply_convert_fusion = bf16[2,256,4096]{2,1,0:T(8,128)(2,1)S(1)} fusion(f32[2,4096]{1,0:T(2,128)S(1)} %multiply_add_fusion, f32[256,4096]{1,0:T(8,128)S(1)} %fusion.7, f32[4096]{0:T(1024)S(1)} %fusion.9, pred[2,256]{1,0:T(4,128)(4,1)S(1)} %slice_compare_fusion), kind=kLoop, calls=%fused_computation | loop fusion | flops 6291456 | bytes 8438272 | tf_op jit(solution)/shard_map/convert.2
  24.9 3.7 %pad_maximum_fusion = bf16[3,256,4096]{2,1,0:T(8,128)(2,1)} fusion(bf16[2,256,4096]{2,1,0:T(8,128)(2,1)S(1)} %multiply_convert_fusion, bf16[1,256,4096]{2,1,0:T(8,128)(2,1)S(1)} %copy-done.2), kind=kLoop, calls=%fused_computation.1 | loop fusion | flops 3145728 | bytes 12582912 | tf_op jit(solution)/shard_map/concatenate | solution.py:384
  28.6 0.1 copy-done.3
  28.7 0.9 copy-done.4
  29.6 8.4 %fusion = f32[768,768]{0,1:T(8,128)S(1)} fusion(bf16[768,4096]{1,0:T(8,128)(2,1)} %bitcast.17, bf16[4096,128]{1,0:T(8,128)(2,1)S(1)} %get-tuple-element.6, bf16[4096,128]{1,0:T(8,128)(2,1)S(1)} %copy-done.4, bf16[4096,512]{1,0:T(8,128)(2,1)S(1)} %copy-done.3), kind=kOutput, calls=%fused_computation.2 | convolution fusion | flops 4850712576 | bytes 14942208 | tf_op jit(solution)/shard_map/dot_general | solution.py:385
  38.1 1.3 slice.23
  39.4 0.1 multiply_convert_fusion.2
  39.5 0.2 copy.18
  39.7 1.9 %copy.20.raw_ref = f32[768,512]{1,0:T(8,128)S(1)} copy(f32[768,512]{0,1:T(8,128)} %slice.23) | data formatting | bytes 3145728
  41.6 71.7 %shard_map.140.att_ref = bf16[768,512]{1,0:T(8,128)(2,1)S(1)} custom-call(f32[768,512]{1,0:T(8,128)S(1)} %copy.20.raw_ref, f32[1,128]{1,0:T(1,128)S(1)} %bitcast.14, bf16[3,256,256]{2,1,0:T(8,128)(2,1)S(1)} %bitcast.12), custom_call_target="tpu_custom_call" | custom-call | tf_op jit(solution)/shard_map/pallas_call | solution.py:188
  113.3 26.3 %shard_map.141 = (bf16[256,2048]{1,0:T(8,128)(2,1)S(1)}, bf16[256,2048]{1,0:T(8,128)(2,1)S(1)}) custom-call(bf16[768,512]{1,0:T(8,128)(2,1)S(1)} %shard_map.140.att_ref, bf16[1024,4096]{1,0:T(8,128)(2,1)} %w_out_ref.1, f32[256,1]{1,0:T(8,128)S(1)} %convert_element_type.48.live_ref), custom_call_target="tpu_custom_call" | custom-call | tf_op jit(solution)/shard_map/pallas_call | solution.py:294
  139.6 1.0 copy.24
  140.6 1.0 copy.25
  (34 shorter events, 0.2 us)
Async XLA Ops:
  1.7 14.5 %collective-permute-start = (bf16[128,2048]{1,0:T(8,128)(2,1)S(1)}, bf16[128,2048]{1,0:T(8,128)(2,1)S(1)}, u32[]{:S(2)}, u32[]{:S(2)}) collective-permute-start(bf16[128,2048]{1,0:T(8,128)(2,1)S(1)} %constant_dynamic-slice_fusion.3), channel_id=1, source_target_pairs={{0,64},{64,0},{1,65},{65,1},{2,66},{66,2},{3,67},{67,3},{4,68},{68... | collective-permute-start | bytes 1572872 | tf_op jit(solution)/shard_map/ppermute | solution.py:357
  5.9 10.2 %collective-permute-start.2 = (s32[1,257]{1,0:T(1,128)S(1)}, s32[1,257]{1,0:T(1,128)S(1)}, u32[]{:S(2)}, u32[]{:S(2)}) collective-permute-start(s32[1,257]{1,0:T(1,128)S(1)} %pad_add_fusion), channel_id=1, source_target_pairs={{0,64},{64,0},{1,65},{65,1},{2,66},{66,2},{3,67},{67,3},{4,68},{68... | collective-permute-start | bytes 3092 | tf_op jit(solution)/shard_map/ppermute | solution.py:356
  8.1 4.7 %copy-start.5 = (bf16[4096,256]{1,0:T(8,128)(2,1)S(1)}, bf16[4096,256]{1,0:T(8,128)(2,1)}, u32[]{:S(2)}) copy-start(bf16[4096,256]{1,0:T(8,128)(2,1)} %param.19) | copy-start | bytes 6291460
  8.1 4.7 %copy-start.6 = (bf16[4096,256]{1,0:T(8,128)(2,1)S(1)}, bf16[4096,256]{1,0:T(8,128)(2,1)}, u32[]{:S(2)}) copy-start(bf16[4096,256]{1,0:T(8,128)(2,1)} %param.18) | copy-start | bytes 6291460
  12.8 1.2 copy-start.7
  12.8 1.2 copy-start.8
  12.8 1.2 copy-start.12
  12.8 3.3 %copy-start.10 = (s32[1,256]{1,0:T(1,128)S(1)}, s32[1,256]{1,0:T(1,128)}, u32[]{:S(2)}) copy-start(s32[1,256]{1,0:T(1,128)} %param.23) | copy-start | bytes 3076
  12.8 5.1 %copy-start.9 = (f32[4096]{0:T(1024)S(1)}, f32[4096]{0:T(1024)}, u32[]{:S(2)}) copy-start(f32[4096]{0:T(1024)} %param.16) | copy-start | bytes 49156
  12.8 6.9 %copy-start.1 = (bf16[256,2048]{1,0:T(8,128)(2,1)S(1)}, bf16[256,2048]{1,0:T(8,128)(2,1)}, u32[]{:S(2)}) copy-start(bf16[256,2048]{1,0:T(8,128)(2,1)} %param.13) | copy-start | bytes 3145732
  16.3 3.2 %collective-permute-start.1 = (bf16[128,2048]{1,0:T(8,128)(2,1)S(1)}, bf16[128,2048]{1,0:T(8,128)(2,1)S(1)}, u32[]{:S(2)}, u32[]{:S(2)}) collective-permute-start(bf16[128,2048]{1,0:T(8,128)(2,1)S(1)} %collective-permute-done), channel_id=1, source_target_pairs={{0,1},{1,0},{2,3},{3,2},{4,5},{5,4},{6,7},{7,6},{8,9},{9,8},{10,11... | collective-permute-start | bytes 1572872 | tf_op jit(solution)/shard_map/ppermute | solution.py:360
  23.2 1.7 %copy-start.2 = (bf16[1,256,4096]{2,1,0:T(8,128)(2,1)S(1)}, bf16[1,256,4096]{2,1,0:T(8,128)(2,1)}, u32[]{:S(2)}) copy-start(bf16[1,256,4096]{2,1,0:T(8,128)(2,1)} %multiply_convert_fusion.1) | copy-start | bytes 6291460
  24.9 3.9 %copy-start.3 = (bf16[4096,512]{1,0:T(8,128)(2,1)S(1)}, bf16[4096,512]{1,0:T(8,128)(2,1)}, u32[]{:S(2)}) copy-start(bf16[4096,512]{1,0:T(8,128)(2,1)} %constant_dynamic-slice_fusion.2) | copy-start | bytes 12582916
  24.9 4.7 %copy-start.4 = (bf16[4096,128]{1,0:T(8,128)(2,1)S(1)}, bf16[4096,128]{1,0:T(8,128)(2,1)}, u32[]{:S(2)}) copy-start(bf16[4096,128]{1,0:T(8,128)(2,1)} %get-tuple-element.7) | copy-start | bytes 3145732
  29.6 9.8 %copy-start.11 = (f32[128]{0:T(128)S(1)}, f32[128]{0:T(128)}, u32[]{:S(2)}) copy-start(f32[128]{0:T(128)} %param.22) | copy-start | bytes 1540
  38.1 3.5 %copy-start = (f32[128]{0:T(128)S(1)}, f32[128]{0:T(128)}, u32[]{:S(2)}) copy-start(f32[128]{0:T(128)} %param.21) | copy-start | bytes 1540

commit v6 on v5

--- a/solution.py
+++ b/solution.py
@@ -13,6 +13,7 @@
 TSTEPS = 1000
 EPS = 1e-06
 GROUP = 4
+SIDE = 4
 MESH = pl.DeviceIdType.MESH
 
 
@@ -68,16 +69,20 @@
         def _():
             act(push(partner))
 
-        def to_pair(index, carry):
-            act(push(2 * index + lane))
-
-            @pl.when(jnp.logical_not(relayed(pair)))
+        def to_pair(step, carry):
+            index = SIDE * (SIDE - 1 - step // SIDE) + lax.rem(pair + 1 + lax.rem(step, SIDE), SIDE)
+
+            @pl.when(index > pair)
+            def _():
+                act(push(2 * index + lane))
+
+            @pl.when(jnp.logical_and(index > pair, jnp.logical_not(relayed(pair))))
             def _():
                 act(push(2 * index + 1 - lane))
 
             return carry
 
-        lax.fori_loop(pair + 1, spans // 2, to_pair, 0)
+        lax.fori_loop(0, SIDE * SIDE, to_pair, 0)
 
     def forward(index):
         slot = 2 * index + lane
@@ -363,9 +368,9 @@
         jnp.concatenate([near_rows, far_rows], axis=0),
         jnp.concatenate([far_rows, near_rows], axis=0),
     )
-    weights = jnp.concatenate(
+    query_weight = lax.dynamic_slice_in_dim(w_query, mine * q_width, q_width, axis=1)
+    pair_weight = jnp.concatenate(
         [
-            lax.dynamic_slice_in_dim(w_query, mine * q_width, q_width, axis=1),
             lax.dynamic_slice_in_dim(w_key, mine * HD, HD, axis=1),
             lax.dynamic_slice_in_dim(w_value, mine * HD, HD, axis=1),
         ],
@@ -380,15 +385,15 @@
     condition = (
         1.0 + both_notes[:, rows:].astype(jnp.float32)[:, :, None] / TSTEPS * time_shift[None, None, :]
     )
-    noisy = jnp.where(both_notes[:, :rows, None] == 1, mask_base[None], base[None]) * condition
-    all_rows = jnp.concatenate([base[None], noisy], axis=0).astype(jnp.bfloat16)
-    wide = jnp.dot(
-        all_rows.reshape(streams * rows, -1), weights, preferred_element_type=jnp.float32
-    )
-    raw = wide[:, :q_width]
-    key_wide = wide[:, q_width : q_width + HD]
+    condition = jnp.concatenate([jnp.ones_like(condition[:1]), condition], axis=0)
+    hidden = jnp.concatenate([jnp.zeros_like(masked), both_notes[:, :rows]], axis=0)
+    all_rows = jnp.where(hidden[:, :, None] == 1, mask_base[None], base[None]) * condition
+    all_rows = all_rows.astype(jnp.bfloat16).reshape(streams * rows, -1)
+    raw = jnp.dot(all_rows, query_weight, preferred_element_type=jnp.float32)
+    wide = jnp.dot(all_rows, pair_weight, preferred_element_type=jnp.float32)
+    key_wide = wide[:, :HD]
     keys = (key_wide * inverse_rms(key_wide) * k_gain).astype(jnp.bfloat16)
-    values = wide[:, q_width + HD :].astype(jnp.bfloat16)
+    values = wide[:, HD:].astype(jnp.bfloat16)
     own = jnp.concatenate([keys, values], axis=1).reshape(streams, rows, 2 * HD)
     spans = lax.axis_size("ctx")
     attended = attend(raw, q_gain[None, :], own, streams, rows, heads, spans)

time: 142 us -> 138 us (0.972)
  local copies, waits for them, and re-layouts: 13.4 us -> 6.65 us
  waiting for transfers between devices: 3.33 us -> 7.43 us
  other arithmetic: 11.5 us -> 9.49 us
    dynamic_slice x1 -> x0, local copies, waits for them, and re-layouts: 4.65 us -> none  [on_device(): lax.dynamic_slice_in_dim(w_query, mine * q_width, q_width, axis=1)]
    concatenate x1 -> x0, other arithmetic: 3.74 us -> none  [on_device(): all_rows = jnp.concatenate([base[None], noisy], axis=0).astype(jnp.bfloat16)]
    ppermute x1, waiting for transfers between devices: 1.89 us -> 5.6 us  [on_device(): other_notes = lax.ppermute(notes, 'copy', SWAP)]
    another operation x2 -> x0, other arithmetic: 3.62 us -> none
    convert_element_type x0 -> x1, other arithmetic: none -> 2.92 us  [on_device(): all_rows = all_rows.astype(jnp.bfloat16).reshape(streams * rows, -1)]
    unnamed x29 -> x18, local copies, waits for them, and re-layouts: 4.88 us -> 2.57 us
    select_n x1, other arithmetic: 0.25 us -> 1.91 us  [on_device(): jnp.where(core == 0, jnp.concatenate([near_rows, far_rows], axis=0), jnp....]
    dot_general x1 -> x2, matrix products: 8.4 us -> 8.79 us  [the longest x1 6.75 us: on_device(): raw = jnp.dot(all_rows, query_weight, preferred_element_type=jnp.float32)]
  transfers between devices with their start and end apart: 3 -> 3, of which waited for: 2 -> 2; matrix products, arithmetic and copies ran while one was open for 6% -> 4% of each run, Pallas kernels for 0% -> 0%
where the time goes in v6:
time: 138 us; the launch traced here: 137 us
  Pallas kernels  98.1 us (71%)
  other arithmetic  9.49 us (7%)
  matrix products  8.79 us (6%)
  waiting for transfers between devices  7.43 us (5%)
  local copies, waits for them, and re-layouts  6.65 us (5%)
  starting transfers between devices  4.58 us (3%)
  between operations  2.23 us (2%)
    pallas_call x1, Pallas kernels, attend(): pl.pallas_call(functools.partial(attend_kernel, rows, heads, streams, spa...  71.7 us
    pallas_call x1, Pallas kernels, project(): pl.pallas_call(functools.partial(project_kernel, rows), out_shape=(out, o...  26.4 us
    dot_general x1, matrix products, on_device(): raw = jnp.dot(all_rows, query_weight, preferred_element_type=jnp.float32)  6.75 us
    ppermute x1, waiting for transfers between devices, on_device(): other_notes = lax.ppermute(notes, 'copy', SWAP)  5.6 us
    convert_element_type x1, other arithmetic, on_device(): all_rows = all_rows.astype(jnp.bfloat16).reshape(streams * rows, -1)  2.92 us
  transfers between devices with their start and end apart: 3, of which 2 were waited for; matrix products, arithmetic and copies ran while one was open for 4% of the time, Pallas kernels for 0%

profile of v6, /device:TPU:121, one launch (start us, length us, event | category | flops | bytes accessed | tf_op | source)
XLA Modules:
  0.0 137.3 jit_solution(14234887789604146512)
XLA Ops:
  0.6 0.0 copy-start.5
  0.7 0.0 copy-start.3
  0.7 2.0 %constant_dynamic-slice_fusion.2 = bf16[128,2048]{1,0:T(8,128)(2,1)} fusion(bf16[256,2048]{1,0:T(8,128)(2,1)} %param.13, s32[]{:T(128)S(6)} %select_n.50), kind=kLoop, calls=%fused_computation.36 | loop fusion | bytes 1048580 | tf_op jit(solution)/shard_map/dynamic_slice | solution.py:363
  2.7 2.7 %collective-permute-start.1 = (bf16[128,2048]{1,0:T(8,128)(2,1)}, bf16[128,2048]{1,0:T(8,128)(2,1)}, u32[]{:S(2)}, u32[]{:S(2)}) collective-permute-start(bf16[128,2048]{1,0:T(8,128)(2,1)} %constant_dynamic-slice_fusion.2), channel_id=1, source_target_pairs={{0,64},{64,0},{1,65},{65,1},{2,66},{66,2},{3,67},{67,3},{4,68},{68... | collective-permute-start | bytes 1572872 | tf_op jit(solution)/shard_map/ppermute | solution.py:362
  6.0 0.7 pad_add_fusion
  6.7 0.2 collective-permute-start
  7.0 1.4 %fusion.9 = f32[]{:T(128)} fusion(bf16[4096]{0:T(1024)(128)(2,1)} %param.15), kind=kLoop, calls=%fused_computation.23 | loop fusion | flops 12287 | bytes 8196 | tf_op jit(solution)/shard_map/reduce_sum | solution.py:21
  9.0 0.7 fusion.10
  9.7 1.7 %constant_dynamic-slice_fusion = (bf16[4096,128]{1,0:T(8,128)(2,1)S(1)}, bf16[4096,128]{1,0:T(8,128)(2,1)S(1)}) fusion(bf16[4096,256]{1,0:T(8,128)(2,1)} %param.19, s32[]{:T(128)S(6)} %select_n.55, bf16[4096,256]{1,0:T(8,128)(2,1)} %param.18), kind=kLoop, calls=%fused_computation.33 | loop fusion | bytes 4194308 | tf_op jit(solution)/shard_map/dynamic_slice | solution.py:375
  11.5 0.1 broadcast_in_dim.61
  11.5 0.1 convert_element_type.40.live_ref
  11.7 5.6 %collective-permute-done = s32[1,257]{1,0:T(1,128)S(1)} collective-permute-done((s32[1,257]{1,0:T(1,128)S(1)}, s32[1,257]{1,0:T(1,128)S(1)}, u32[]{:S(2)}, u32[]{:S(2)}) %collective-permute-start) | collective-permute-done | bytes 1060 | tf_op jit(solution)/shard_map/ppermute | solution.py:361
  17.3 0.1 fusion.12
  17.4 0.1 multiply_add_fusion
  17.5 0.0 collective-permute-done.1
  17.5 1.6 %collective-permute-start.2 = (bf16[128,2048]{1,0:T(8,128)(2,1)}, bf16[128,2048]{1,0:T(8,128)(2,1)}, u32[]{:S(2)}, u32[]{:S(2)}) collective-permute-start(bf16[128,2048]{1,0:T(8,128)(2,1)} %collective-permute-done.1), channel_id=1, source_target_pairs={{0,1},{1,0},{2,3},{3,2},{4,5},{5,4},{6,7},{7,6},{8,9},{9,8},{10,11... | collective-permute-start | bytes 1572872 | tf_op jit(solution)/shard_map/ppermute | solution.py:365
  19.2 1.8 %collective-permute-done.2 = bf16[128,2048]{1,0:T(8,128)(2,1)} collective-permute-done((bf16[128,2048]{1,0:T(8,128)(2,1)}, bf16[128,2048]{1,0:T(8,128)(2,1)}, u32[]{:S(2)}, u32[]{:S(2)}) %collective-permute-start.2) | collective-permute-done | bytes 524320 | tf_op jit(solution)/shard_map/ppermute | solution.py:365
  21.0 1.9 %maximum_select_fusion.1 = bf16[256,2048]{1,0:T(8,128)(2,1)S(1)} fusion(bf16[128,2048]{1,0:T(8,128)(2,1)} %collective-permute-done.2, bf16[128,2048]{1,0:T(8,128)(2,1)} %collective-permute-done.1, pred[]{:T(512)S(6)} %eq.16), kind=kLoop, calls=%fused_computation.14 | loop fusion | flops 4718592 | bytes 2097153 | tf_op jit(solution)/shard_map/jit(_where)/select_n | solution.py:366
  23.0 0.6 fusion.1
  23.6 0.8 fusion.2
  24.5 2.9 %fusion = bf16[768,4096]{1,0:T(8,128)(2,1)S(1)} fusion(f32[3,4096]{1,0:T(4,128)S(1)} %pad_bitcast_fusion, f32[256,4096]{1,0:T(8,128)S(1)} %fusion.2, f32[4096]{0:T(1024)S(1)} %fusion.10, pred[768]{0:T(1024)(128)(4,1)S(1)} %broadcast_in_dim.55), kind=kLoop, calls=%fused_computation.1 | loop fusion | flops 9437184 | bytes 10552064 | tf_op jit(solution)/shard_map/convert_element_type | solution.py:391
  27.4 0.0 copy-start.6
  27.4 2.0 %fusion.5 = f32[768,256]{0,1:T(8,128)S(1)} fusion(bf16[768,4096]{1,0:T(8,128)(2,1)S(1)} %fusion, bf16[4096,128]{1,0:T(8,128)(2,1)S(1)} %get-tuple-element.6, bf16[4096,128]{1,0:T(8,128)(2,1)S(1)} %get-tuple-element.7), kind=kOutput, calls=%fused_computation.10 | convolution fusion | flops 1614807040 | bytes 9175040 | tf_op jit(solution)/shard_map/dot_general | solution.py:393
  29.4 0.6 copy-done.2
  30.1 0.1 multiply_convert_fusion
  30.3 0.2 copy.16
  30.4 0.0 copy-start
  30.4 6.8 %fusion.3.raw_ref = f32[768,512]{1,0:T(8,128)S(1)} fusion(bf16[768,4096]{1,0:T(8,128)(2,1)} %copy-done.2, bf16[4096,1024]{1,0:T(8,128)(2,1)} %param.17, s32[]{:T(128)S(6)} %select_n.54), kind=kOutput, calls=%fused_computation.7 | convolution fusion | flops 3221225472 | bytes 12058628 | tf_op jit(solution)/shard_map/dot_general | solution.py:392
  37.2 71.7 %shard_map.140.att_ref = bf16[768,512]{1,0:T(8,128)(2,1)S(1)} custom-call(f32[768,512]{1,0:T(8,128)S(1)} %fusion.3.raw_ref, f32[1,128]{1,0:T(1,128)S(1)} %bitcast.22, bf16[3,256,256]{2,1,0:T(8,128)(2,1)S(1)} %bitcast.20), custom_call_target="tpu_custom_call" | custom-call | tf_op jit(solution)/shard_map/pallas_call | solution.py:193
  109.0 26.4 %shard_map.141 = (bf16[256,2048]{1,0:T(8,128)(2,1)S(1)}, bf16[256,2048]{1,0:T(8,128)(2,1)S(1)}) custom-call(bf16[768,512]{1,0:T(8,128)(2,1)S(1)} %shard_map.140.att_ref, bf16[1024,4096]{1,0:T(8,128)(2,1)} %w_out_ref.1, f32[256,1]{1,0:T(8,128)S(1)} %convert_element_type.40.live_ref), custom_call_target="tpu_custom_call" | custom-call | tf_op jit(solution)/shard_map/pallas_call | solution.py:299
  135.4 1.0 copy.21
  136.3 1.0 copy.22
  (23 shorter events, 0.2 us)
Async XLA Ops:
  0.6 22.3 %copy-start.1 = (bf16[256,2048]{1,0:T(8,128)(2,1)S(1)}, bf16[256,2048]{1,0:T(8,128)(2,1)}, u32[]{:S(2)}) copy-start(bf16[256,2048]{1,0:T(8,128)(2,1)} %param.13) | copy-start | bytes 3145732
  0.6 16.7 %copy-start.5 = (s32[1,256]{1,0:T(1,128)S(1)}, s32[1,256]{1,0:T(1,128)}, u32[]{:S(2)}) copy-start(s32[1,256]{1,0:T(1,128)} %param.23) | copy-start | bytes 3076
  0.7 10.8 %copy-start.3 = (bf16[4096]{0:T(1024)(128)(2,1)S(1)}, bf16[4096]{0:T(1024)(128)(2,1)}, u32[]{:S(2)}) copy-start(bf16[4096]{0:T(1024)(128)(2,1)} %param.14) | copy-start | bytes 24580
  0.7 10.8 %copy-start.7 = (s32[1,4]{1,0:T(1,128)S(1)}, s32[1,4]{1,0:T(1,128)}, u32[]{:S(2)}) copy-start(s32[1,4]{1,0:T(1,128)} %param.24) | copy-start | bytes 52
  0.7 16.8 %copy-start.4 = (f32[4096]{0:T(1024)S(1)}, f32[4096]{0:T(1024)}, u32[]{:S(2)}) copy-start(f32[4096]{0:T(1024)} %param.16) | copy-start | bytes 49156
  2.7 14.9 %collective-permute-start.1 = (bf16[128,2048]{1,0:T(8,128)(2,1)}, bf16[128,2048]{1,0:T(8,128)(2,1)}, u32[]{:S(2)}, u32[]{:S(2)}) collective-permute-start(bf16[128,2048]{1,0:T(8,128)(2,1)} %constant_dynamic-slice_fusion.2), channel_id=1, source_target_pairs={{0,64},{64,0},{1,65},{65,1},{2,66},{66,2},{3,67},{67,3},{4,68},{68... | collective-permute-start | bytes 1572872 | tf_op jit(solution)/shard_map/ppermute | solution.py:362
  6.7 10.6 %collective-permute-start = (s32[1,257]{1,0:T(1,128)S(1)}, s32[1,257]{1,0:T(1,128)S(1)}, u32[]{:S(2)}, u32[]{:S(2)}) collective-permute-start(s32[1,257]{1,0:T(1,128)S(1)} %pad_add_fusion), channel_id=1, source_target_pairs={{0,64},{64,0},{1,65},{65,1},{2,66},{66,2},{3,67},{67,3},{4,68},{68... | collective-permute-start | bytes 3092 | tf_op jit(solution)/shard_map/ppermute | solution.py:361
  17.5 3.5 %collective-permute-start.2 = (bf16[128,2048]{1,0:T(8,128)(2,1)}, bf16[128,2048]{1,0:T(8,128)(2,1)}, u32[]{:S(2)}, u32[]{:S(2)}) collective-permute-start(bf16[128,2048]{1,0:T(8,128)(2,1)} %collective-permute-done.1), channel_id=1, source_target_pairs={{0,1},{1,0},{2,3},{3,2},{4,5},{5,4},{6,7},{7,6},{8,9},{9,8},{10,11... | collective-permute-start | bytes 1572872 | tf_op jit(solution)/shard_map/ppermute | solution.py:365
  27.4 2.7 %copy-start.2 = (bf16[768,4096]{1,0:T(8,128)(2,1)}, bf16[768,4096]{1,0:T(8,128)(2,1)S(1)}, u32[]{:S(2)}) copy-start(bf16[768,4096]{1,0:T(8,128)(2,1)S(1)} %fusion) | copy-start | bytes 18874372
  27.4 2.7 %copy-start.6 = (f32[128]{0:T(128)S(1)}, f32[128]{0:T(128)}, u32[]{:S(2)}) copy-start(f32[128]{0:T(128)} %param.22) | copy-start | bytes 1540
  30.4 6.8 %copy-start = (f32[128]{0:T(128)S(1)}, f32[128]{0:T(128)}, u32[]{:S(2)}) copy-start(f32[128]{0:T(128)} %param.21) | copy-start | bytes 1540

commit v7 on v6

--- a/solution.py
+++ b/solution.py
@@ -22,7 +22,8 @@
 
 
 def attend_kernel(
-    rows, heads, streams, spans, raw_ref, gain_ref, own_ref, out_ref, kv_ref, q_ref, acc_ref, send_sem, recv_sem, forward_sem
+    rows, heads, streams, spans, row_ref, w_query_ref, gain_ref, own_ref, out_ref,
+    weight_ref, kv_ref, q_ref, acc_ref, send_sem, recv_sem, forward_sem, load_sem,
 ):
     me = lax.axis_index("ctx")
 
@@ -112,6 +113,8 @@
 
         return carry
 
+    load = pltpu.make_async_copy(w_query_ref, weight_ref, load_sem)
+    load.start()
     each_push(lambda copy: copy.start())
     scale = math.log2(math.e) / math.sqrt(HD)
     gain = gain_ref[...]
@@ -128,12 +131,18 @@
         )
         return jnp.exp2(scores * scale)
 
+    load.wait()
     keys, values = split(own_ref[0])
     for stream in range(streams):
         if stream:
             self_keys, self_values = split(own_ref[stream])
+        wide = jnp.dot(
+            row_ref[stream * rows : (stream + 1) * rows],
+            weight_ref[...],
+            preferred_element_type=jnp.float32,
+        )
         for head in range(heads):
-            raw = raw_ref[stream * rows : (stream + 1) * rows, head * HD : (head + 1) * HD]
+            raw = wide[:, head * HD : (head + 1) * HD]
             queries = (raw * inverse_rms(raw) * gain).astype(jnp.bfloat16)
             at = pl.ds((stream * heads + head) * rows, rows)
             q_ref[at] = queries
@@ -189,24 +198,31 @@
     lax.fori_loop(0, pair, end_relay, 0)
 
 
-def attend(raw, q_gain, own, streams, rows, heads, spans):
+def attend(all_rows, query_weight, q_gain, own, streams, rows, heads, spans):
     return pl.pallas_call(
         functools.partial(attend_kernel, rows, heads, streams, spans),
         out_shape=jax.ShapeDtypeStruct((streams * rows, heads * HD), jnp.bfloat16),
-        in_specs=[pl.BlockSpec(memory_space=pltpu.VMEM)] * 3,
+        in_specs=[
+            pl.BlockSpec(memory_space=pltpu.VMEM),
+            pl.BlockSpec(memory_space=pltpu.HBM),
+            pl.BlockSpec(memory_space=pltpu.VMEM),
+            pl.BlockSpec(memory_space=pltpu.VMEM),
+        ],
         out_specs=pl.BlockSpec(memory_space=pltpu.VMEM),
         scratch_shapes=[
+            pltpu.VMEM(query_weight.shape, jnp.bfloat16),
             pltpu.VMEM((spans, rows, 2 * HD), jnp.bfloat16),
             pltpu.VMEM((streams * heads * rows, HD), jnp.bfloat16),
             pltpu.VMEM((streams * heads * rows, 2 * HD), jnp.float32),
             pltpu.SemaphoreType.DMA((spans,)),
             pltpu.SemaphoreType.DMA((spans,)),
             pltpu.SemaphoreType.DMA((spans,)),
+            pltpu.SemaphoreType.DMA,
         ],
         compiler_params=pltpu.CompilerParams(
             vmem_limit_bytes=48 * 2**20, collective_id=0, has_side_effects=True
         ),
-    )(raw, q_gain, own)
+    )(all_rows, query_weight, q_gain, own)
 
 
 def project_kernel(
@@ -389,14 +405,13 @@
     hidden = jnp.concatenate([jnp.zeros_like(masked), both_notes[:, :rows]], axis=0)
     all_rows = jnp.where(hidden[:, :, None] == 1, mask_base[None], base[None]) * condition
     all_rows = all_rows.astype(jnp.bfloat16).reshape(streams * rows, -1)
-    raw = jnp.dot(all_rows, query_weight, preferred_element_type=jnp.float32)
     wide = jnp.dot(all_rows, pair_weight, preferred_element_type=jnp.float32)
     key_wide = wide[:, :HD]
     keys = (key_wide * inverse_rms(key_wide) * k_gain).astype(jnp.bfloat16)
     values = wide[:, HD:].astype(jnp.bfloat16)
     own = jnp.concatenate([keys, values], axis=1).reshape(streams, rows, 2 * HD)
     spans = lax.axis_size("ctx")
-    attended = attend(raw, q_gain[None, :], own, streams, rows, heads, spans)
+    attended = attend(all_rows, query_weight, q_gain[None, :], own, streams, rows, heads, spans)
     live_rows = jnp.repeat(block_live[0], BLK)[:, None].astype(jnp.float32)
     clean_out, noised_out = project(attended, w_out, live_rows)
     noised_out = noised_out[None]

time: 138 us -> 137 us (level)
  matrix products: 8.79 us -> 2.03 us
  local copies, waits for them, and re-layouts: 6.65 us -> 12.4 us
  waiting for transfers between devices: 7.43 us -> 3.76 us
  Pallas kernels: 98.1 us -> 101 us
    dot_general x1 -> x0, matrix products: 6.75 us -> none  [on_device(): raw = jnp.dot(all_rows, query_weight, preferred_element_type=jnp.float32)]
    dynamic_slice x0 -> x1, local copies, waits for them, and re-layouts: none -> 4.64 us  [on_device(): lax.dynamic_slice_in_dim(w_query, mine * q_width, q_width, axis=1)]
    ppermute x1, waiting for transfers between devices: 5.6 us -> 1.93 us  [on_device(): other_notes = lax.ppermute(notes, 'copy', SWAP)]
    pallas_call x1, Pallas kernels: 71.7 us -> 74.6 us  [attend(): pl.pallas_call(functools.partial(attend_kernel, rows, heads, streams, spa...]
    unnamed x18 -> x24, local copies, waits for them, and re-layouts: 2.57 us -> 5.26 us
    dynamic_slice x1, local copies, waits for them, and re-layouts: 1.68 us -> 0.15 us  [on_device(): lax.dynamic_slice_in_dim(w_value, mine * HD, HD, axis=1)]
  transfers between devices with their start and end apart: 3 -> 3, of which waited for: 2 -> 2; matrix products, arithmetic and copies ran while one was open for 4% -> 6% of each run, Pallas kernels for 0% -> 0%
where the time goes in v7:
time: 137 us; the launch traced here: 135 us
  Pallas kernels  101 us (74%)
  local copies, waits for them, and re-layouts  12.4 us (9%)
  other arithmetic  9.52 us (7%)
  starting transfers between devices  4.58 us (3%)
  waiting for transfers between devices  3.76 us (3%)
  between operations  2.23 us (2%)
  matrix products  2.03 us (1%)
    pallas_call x1, Pallas kernels, attend(): pl.pallas_call(functools.partial(attend_kernel, rows, heads, streams, spa...  74.6 us
    pallas_call x1, Pallas kernels, project(): pl.pallas_call(functools.partial(project_kernel, rows), out_shape=(out, o...  26.4 us
    unnamed x24, local copies, waits for them, and re-layouts  5.26 us
    dynamic_slice x1, local copies, waits for them, and re-layouts, on_device(): lax.dynamic_slice_in_dim(w_query, mine * q_width, q_width, axis=1)  4.64 us
    convert_element_type x1, other arithmetic, on_device(): all_rows = all_rows.astype(jnp.bfloat16).reshape(streams * rows, -1)  2.93 us
    ppermute x1, starting transfers between devices, on_device(): lax.ppermute(lax.dynamic_slice_in_dim(clean_tokens, core * (rows // 2), r...  2.74 us
  transfers between devices with their start and end apart: 3, of which 2 were waited for; matrix products, arithmetic and copies ran while one was open for 6% of the time, Pallas kernels for 0%

profile of v7, /device:TPU:121, one launch (start us, length us, event | category | flops | bytes accessed | tf_op | source)
XLA Modules:
  0.0 135.5 jit_solution(2273530392856772449)
XLA Ops:
  0.6 1.9 %constant_dynamic-slice_fusion.3 = bf16[128,2048]{1,0:T(8,128)(2,1)} fusion(bf16[256,2048]{1,0:T(8,128)(2,1)} %param.13, s32[]{:T(128)S(6)} %select_n.50), kind=kLoop, calls=%fused_computation.34 | loop fusion | bytes 1048580 | tf_op jit(solution)/shard_map/dynamic_slice | solution.py:379
  2.5 2.7 %collective-permute-start.1 = (bf16[128,2048]{1,0:T(8,128)(2,1)}, bf16[128,2048]{1,0:T(8,128)(2,1)}, u32[]{:S(2)}, u32[]{:S(2)}) collective-permute-start(bf16[128,2048]{1,0:T(8,128)(2,1)} %constant_dynamic-slice_fusion.3), channel_id=1, source_target_pairs={{0,64},{64,0},{1,65},{65,1},{2,66},{66,2},{3,67},{67,3},{4,68},{68... | collective-permute-start | bytes 1572872 | tf_op jit(solution)/shard_map/ppermute | solution.py:378
  5.9 0.7 pad_add_fusion
  6.6 0.2 collective-permute-start
  6.8 1.4 %fusion.7 = f32[]{:T(128)} fusion(bf16[4096]{0:T(1024)(128)(2,1)} %param.15), kind=kLoop, calls=%fused_computation.21 | loop fusion | flops 12287 | bytes 8196 | tf_op jit(solution)/shard_map/reduce_sum | solution.py:21
  8.9 0.7 fusion.8
  9.6 4.6 %constant_dynamic-slice_fusion.2.w_query_ref = bf16[4096,512]{1,0:T(8,128)(2,1)} fusion(bf16[4096,1024]{1,0:T(8,128)(2,1)} %param.17, s32[]{:T(128)S(6)} %select_n.54), kind=kLoop, calls=%fused_computation.33 | loop fusion | bytes 8388612 | tf_op jit(solution)/shard_map/dynamic_slice | solution.py:387
  14.3 0.0 copy-start.8
  14.3 0.1 constant_dynamic-slice_fusion
  14.5 0.5 copy-done.10
  15.0 0.1 copy-done.6
  15.0 0.1 broadcast_in_dim.61
  15.1 0.1 convert_element_type.40.live_ref
  15.2 1.9 %collective-permute-done = s32[1,257]{1,0:T(1,128)S(1)} collective-permute-done((s32[1,257]{1,0:T(1,128)S(1)}, s32[1,257]{1,0:T(1,128)S(1)}, u32[]{:S(2)}, u32[]{:S(2)}) %collective-permute-start) | collective-permute-done | bytes 1060 | tf_op jit(solution)/shard_map/ppermute | solution.py:377
  17.2 0.1 fusion.10
  17.3 0.1 multiply_add_fusion
  17.4 1.6 %collective-permute-start.2 = (bf16[128,2048]{1,0:T(8,128)(2,1)}, bf16[128,2048]{1,0:T(8,128)(2,1)}, u32[]{:S(2)}, u32[]{:S(2)}) collective-permute-start(bf16[128,2048]{1,0:T(8,128)(2,1)} %collective-permute-done.1), channel_id=1, source_target_pairs={{0,1},{1,0},{2,3},{3,2},{4,5},{5,4},{6,7},{7,6},{8,9},{9,8},{10,11... | collective-permute-start | bytes 1572872 | tf_op jit(solution)/shard_map/ppermute | solution.py:381
  19.1 1.8 %collective-permute-done.2 = bf16[128,2048]{1,0:T(8,128)(2,1)} collective-permute-done((bf16[128,2048]{1,0:T(8,128)(2,1)}, bf16[128,2048]{1,0:T(8,128)(2,1)}, u32[]{:S(2)}, u32[]{:S(2)}) %collective-permute-start.2) | collective-permute-done | bytes 524320 | tf_op jit(solution)/shard_map/ppermute | solution.py:381
  20.9 1.9 %maximum_select_fusion.1 = bf16[256,2048]{1,0:T(8,128)(2,1)S(1)} fusion(bf16[128,2048]{1,0:T(8,128)(2,1)} %collective-permute-done.2, bf16[128,2048]{1,0:T(8,128)(2,1)} %collective-permute-done.1, pred[]{:T(512)S(6)} %eq.16), kind=kLoop, calls=%fused_computation.12 | loop fusion | flops 4718592 | bytes 2097153 | tf_op jit(solution)/shard_map/jit(_where)/select_n | solution.py:382
  22.9 0.6 fusion.1
  23.5 0.8 fusion.2
  24.3 2.9 %fusion.row_ref = bf16[768,4096]{1,0:T(8,128)(2,1)S(1)} fusion(f32[3,4096]{1,0:T(4,128)S(1)} %pad_bitcast_fusion, f32[256,4096]{1,0:T(8,128)S(1)} %fusion.2, f32[4096]{0:T(1024)S(1)} %fusion.8, pred[768]{0:T(1024)(128)(4,1)S(1)} %broadcast_in_dim.55), kind=kLoop, calls=%fused_computation.1 | loop fusion | flops 9437184 | bytes 10552064 | tf_op jit(solution)/shard_map/convert_element_type | solution.py:407
  27.3 0.0 copy-start.9
  27.3 2.0 %fusion.3 = f32[768,256]{0,1:T(8,128)S(1)} fusion(bf16[768,4096]{1,0:T(8,128)(2,1)S(1)} %fusion.row_ref, bf16[4096,128]{1,0:T(8,128)(2,1)S(1)} %get-tuple-element.6, bf16[4096,128]{1,0:T(8,128)(2,1)S(1)} %get-tuple-element.7), kind=kOutput, calls=%fused_computation.8 | convolution fusion | flops 1614807040 | bytes 9175040 | tf_op jit(solution)/shard_map/dot_general | solution.py:408
  29.4 0.6 copy-done.2
  30.0 0.1 multiply_convert_fusion
  30.2 0.2 copy.16
  30.4 2.2 %copy-done = bf16[4096,512]{1,0:T(8,128)(2,1)S(1)} copy-done((bf16[4096,512]{1,0:T(8,128)(2,1)S(1)}, bf16[4096,512]{1,0:T(8,128)(2,1)}, u32[]{:S(2)}) %copy-start) | copy-done | bytes 4194328
  32.5 74.6 %shard_map.140.att_ref = bf16[768,512]{1,0:T(8,128)(2,1)S(1)} custom-call(bf16[768,4096]{1,0:T(8,128)(2,1)} %copy-done.2, bf16[4096,512]{1,0:T(8,128)(2,1)S(1)} %copy-done, f32[1,128]{1,0:T(1,128)S(1)} %bitcast.21, bf16[3,256,256]{2,1,0:T(8,128)(2,1)S(1)} %bitcast.19), custom_call_target="tpu_custom_call" | custom-call | tf_op jit(solution)/shard_map/pallas_call | solution.py:202
  107.1 26.4 %shard_map.141 = (bf16[256,2048]{1,0:T(8,128)(2,1)S(1)}, bf16[256,2048]{1,0:T(8,128)(2,1)S(1)}) custom-call(bf16[768,512]{1,0:T(8,128)(2,1)S(1)} %shard_map.140.att_ref, bf16[1024,4096]{1,0:T(8,128)(2,1)} %w_out_ref.1, f32[256,1]{1,0:T(8,128)S(1)} %convert_element_type.40.live_ref), custom_call_target="tpu_custom_call" | custom-call | tf_op jit(solution)/shard_map/pallas_call | solution.py:315
  133.5 1.0 copy.21
  134.5 1.0 copy.22
  (29 shorter events, 0.2 us)
Async XLA Ops:
  2.5 14.9 %collective-permute-start.1 = (bf16[128,2048]{1,0:T(8,128)(2,1)}, bf16[128,2048]{1,0:T(8,128)(2,1)}, u32[]{:S(2)}, u32[]{:S(2)}) collective-permute-start(bf16[128,2048]{1,0:T(8,128)(2,1)} %constant_dynamic-slice_fusion.3), channel_id=1, source_target_pairs={{0,64},{64,0},{1,65},{65,1},{2,66},{66,2},{3,67},{67,3},{4,68},{68... | collective-permute-start | bytes 1572872 | tf_op jit(solution)/shard_map/ppermute | solution.py:378
  6.6 10.6 %collective-permute-start = (s32[1,257]{1,0:T(1,128)S(1)}, s32[1,257]{1,0:T(1,128)S(1)}, u32[]{:S(2)}, u32[]{:S(2)}) collective-permute-start(s32[1,257]{1,0:T(1,128)S(1)} %pad_add_fusion), channel_id=1, source_target_pairs={{0,64},{64,0},{1,65},{65,1},{2,66},{66,2},{3,67},{67,3},{4,68},{68... | collective-permute-start | bytes 3092 | tf_op jit(solution)/shard_map/ppermute | solution.py:377
  9.6 4.7 %copy-start.4 = (bf16[4096,256]{1,0:T(8,128)(2,1)S(1)}, bf16[4096,256]{1,0:T(8,128)(2,1)}, u32[]{:S(2)}) copy-start(bf16[4096,256]{1,0:T(8,128)(2,1)} %param.19) | copy-start | bytes 6291460
  9.6 4.7 %copy-start.5 = (bf16[4096,256]{1,0:T(8,128)(2,1)S(1)}, bf16[4096,256]{1,0:T(8,128)(2,1)}, u32[]{:S(2)}) copy-start(bf16[4096,256]{1,0:T(8,128)(2,1)} %param.18) | copy-start | bytes 6291460
  14.3 0.7 copy-start.10
  14.3 0.7 copy-start.6
  14.3 2.9 %copy-start.8 = (s32[1,256]{1,0:T(1,128)S(1)}, s32[1,256]{1,0:T(1,128)}, u32[]{:S(2)}) copy-start(s32[1,256]{1,0:T(1,128)} %param.23) | copy-start | bytes 3076
  14.3 3.0 %copy-start.7 = (f32[4096]{0:T(1024)S(1)}, f32[4096]{0:T(1024)}, u32[]{:S(2)}) copy-start(f32[4096]{0:T(1024)} %param.16) | copy-start | bytes 49156
  14.3 8.5 %copy-start.3 = (bf16[256,2048]{1,0:T(8,128)(2,1)S(1)}, bf16[256,2048]{1,0:T(8,128)(2,1)}, u32[]{:S(2)}) copy-start(bf16[256,2048]{1,0:T(8,128)(2,1)} %param.13) | copy-start | bytes 3145732
  17.4 3.5 %collective-permute-start.2 = (bf16[128,2048]{1,0:T(8,128)(2,1)}, bf16[128,2048]{1,0:T(8,128)(2,1)}, u32[]{:S(2)}, u32[]{:S(2)}) collective-permute-start(bf16[128,2048]{1,0:T(8,128)(2,1)} %collective-permute-done.1), channel_id=1, source_target_pairs={{0,1},{1,0},{2,3},{3,2},{4,5},{5,4},{6,7},{7,6},{8,9},{9,8},{10,11... | collective-permute-start | bytes 1572872 | tf_op jit(solution)/shard_map/ppermute | solution.py:381
  27.3 2.7 %copy-start.2 = (bf16[768,4096]{1,0:T(8,128)(2,1)}, bf16[768,4096]{1,0:T(8,128)(2,1)S(1)}, u32[]{:S(2)}) copy-start(bf16[768,4096]{1,0:T(8,128)(2,1)S(1)} %fusion.row_ref) | copy-start | bytes 18874372
  27.3 2.7 %copy-start.9 = (f32[128]{0:T(128)S(1)}, f32[128]{0:T(128)}, u32[]{:S(2)}) copy-start(f32[128]{0:T(128)} %param.22) | copy-start | bytes 1540
  27.3 3.0 %copy-start.1 = (f32[128]{0:T(128)S(1)}, f32[128]{0:T(128)}, u32[]{:S(2)}) copy-start(f32[128]{0:T(128)} %param.21) | copy-start | bytes 1540
  30.3 2.2 %copy-start = (bf16[4096,512]{1,0:T(8,128)(2,1)S(1)}, bf16[4096,512]{1,0:T(8,128)(2,1)}, u32[]{:S(2)}) copy-start(bf16[4096,512]{1,0:T(8,128)(2,1)} %constant_dynamic-slice_fusion.2.w_query_ref) | copy-start | bytes 12582916
